TPU v7x, 32 devices: a whole 2x2x4 slice. The times are simulated.
32 devices in a mesh: band: 4 (over y, core), ma: 8 (over z, x).
Axes of the slice: x: 2, y: 2, z: 4, core: 2. Of those that a mesh axis runs over, the one named last changes fastest.
Arguments:
- sky_maps: bfloat16 [64, 64, 2, 16384], P(None, ('band', 'ma')), may hold values from -6 to 6
- hi_cycles: int32 [64], P(('band', 'ma')), may hold values from 4096 to 8191, as said below
- lo_cycles: int32 [64], P(('band', 'ma')), may hold values from 1024 to 2047, as said below
- azimuth_orders: int32 [128], replicated, may hold values from 0 to 3071, as said below
- legendre_hi: bfloat16 [128, 3072, 64], P(('band', 'ma')), may hold values from -0.75 to 0.75
- legendre_lo: bfloat16 [128, 3072, 64], P(('band', 'ma')), may hold values from -0.109375 to 0.109375
- beam_weights: float32 [3072], replicated, may hold values from 0.05 to 1
Outputs:
- smoothed_maps: float32 [64, 64, 2, 4096], P(None, ('band', 'ma'))
Inputs may be any that keep to these rules, and one draw needn't show every extreme that they name: `hi_cycles`: distinct northern equatorial-belt cycles. `lo_cycles`: distinct northern equatorial-belt cycles. `azimuth_orders`: distinct orders.
All inputs are finite; a program needn't handle non-finite values.
Results may differ from a plain program's by a relative error of at most 0.0038.
Values may be sent and summed in bfloat16 or wider, within the bound.
No kernel may reach another device: no remote copies, remote signals or barrier semaphores. Data moves between devices by JAX's collectives and lax.ppermute only.
A program may use at most 192 MiB of HBM per device.

v0:
```python
import math

import jax
import jax.numpy as jnp
from jax import lax
from jax.sharding import PartitionSpec as P

NSIDE_HI = 4096
NSIDE_LO = 1024
LROWS = 3072
NPIX_HI = 16384
NPIX_LO = 4096


THREE_PASS = lax.Precision.HIGH


def angle_grid(first, second, length):
    product = first[:, None] * second[None, :] % length
    return product.astype(jnp.float32) * (2.0 * math.pi / length)


def cycle_offsets(cycle_ids, side_count):
    return ((cycle_ids - side_count + 1) % 2).astype(jnp.float32)


def per_device(
    sky_maps, hi_cycles, lo_cycles, azimuth_orders, legendre_hi, legendre_lo, beam_weights
):
    map_count = sky_maps.shape[0]
    pair_local = sky_maps.shape[1]
    select_total = azimuth_orders.shape[0]
    owned = legendre_hi.shape[0]
    half_cols = 2 * map_count
    pixels_hi = jnp.arange(NPIX_HI, dtype=jnp.int32)
    angles = angle_grid(pixels_hi, azimuth_orders, NPIX_HI)
    forward_table = jnp.concatenate([jnp.cos(angles), jnp.sin(angles)], axis=1).astype(jnp.bfloat16)
    raw_sums = jnp.dot(
        sky_maps.reshape(-1, NPIX_HI), forward_table, preferred_element_type=jnp.float32
    )
    raw_sums = raw_sums.reshape(map_count, pair_local, 2, 2, select_total)
    real_raw = raw_sums[:, :, :, 0]
    imag_raw = -raw_sums[:, :, :, 1]
    offsets_hi = cycle_offsets(hi_cycles, NSIDE_HI)
    theta_hi = math.pi * offsets_hi[:, None] * azimuth_orders.astype(jnp.float32)[None, :] / NPIX_HI
    cos_hi = jnp.cos(theta_hi)[None, :, None, :]
    sin_hi = jnp.sin(theta_hi)[None, :, None, :]
    scale_hi = 1.0 / math.sqrt(NPIX_HI)
    real_coef = (real_raw * cos_hi + imag_raw * sin_hi) * scale_hi
    imag_coef = (imag_raw * cos_hi - real_raw * sin_hi) * scale_hi
    stacked = jnp.stack([real_coef, imag_coef], axis=3)
    outgoing = (
        jnp.transpose(stacked, (4, 1, 2, 3, 0))
        .reshape(select_total, pair_local, 4 * map_count)
        .astype(jnp.bfloat16)
    )
    owner = lax.axis_index(("band", "ma"))
    own_orders = lax.dynamic_slice_in_dim(azimuth_orders, owner * owned, owned)
    degrees = jnp.arange(LROWS, dtype=jnp.int32)[None, :]
    parity = (degrees + own_orders[:, None]) % 2
    signs_lm = 1.0 - 2.0 * parity.astype(jnp.float32)
    beam_mask = jnp.where(degrees >= own_orders[:, None], beam_weights[None, :], 0.0)
    received = lax.all_to_all(outgoing, ("band", "ma"), split_axis=0, concat_axis=1, tiled=True)
    analysis = jnp.einsum("mlr,mrc->mlc", legendre_hi, received, preferred_element_type=jnp.float32)
    harmonic = analysis[:, :, :half_cols] + signs_lm[..., None] * analysis[:, :, half_cols:]
    weighted = beam_mask[..., None] * harmonic
    paired = jnp.concatenate([weighted, signs_lm[..., None] * weighted], axis=2)
    synthesized = jnp.einsum(
        "mlq,mlc->mqc",
        legendre_lo,
        paired,
        precision=THREE_PASS,
        preferred_element_type=jnp.float32,
    )
    returned = lax.all_to_all(synthesized, ("band", "ma"), split_axis=1, concat_axis=0, tiled=True)
    low_local = returned.shape[1]
    parts_low = returned.reshape(select_total, low_local, 2, 2, map_count)
    real_low = parts_low[:, :, :, 0]
    imag_low = parts_low[:, :, :, 1]
    offsets_lo = cycle_offsets(lo_cycles, NSIDE_LO)
    theta_lo = math.pi * azimuth_orders.astype(jnp.float32)[:, None] * offsets_lo[None, :] / NPIX_LO
    cos_lo = jnp.cos(theta_lo)[:, :, None, None]
    sin_lo = jnp.sin(theta_lo)[:, :, None, None]
    real_rot = real_low * cos_lo - imag_low * sin_lo
    imag_rot = imag_low * cos_lo + real_low * sin_lo
    spectra = jnp.stack([real_rot, imag_rot], axis=0)
    spectra = jnp.transpose(spectra, (4, 2, 3, 0, 1)).reshape(-1, 2 * select_total)
    pixels_lo = jnp.arange(NPIX_LO, dtype=jnp.int32)
    angles_lo = angle_grid(azimuth_orders, pixels_lo, NPIX_LO)
    inverse_table = jnp.concatenate([jnp.cos(angles_lo), -jnp.sin(angles_lo)], axis=0)
    pixels_out = jnp.dot(
        spectra, inverse_table, precision=THREE_PASS, preferred_element_type=jnp.float32
    )
    pixels_out = pixels_out * math.sqrt(2.0 / select_total)
    return pixels_out.reshape(map_count, low_local, 2, NPIX_LO)


def solution(mesh):
    return jax.shard_map(
        per_device,
        mesh=mesh,
        in_specs=(
            P(None, ("band", "ma"), None, None),
            P(("band", "ma")),
            P(("band", "ma")),
            P(),
            P(("band", "ma"), None, None),
            P(("band", "ma"), None, None),
            P(),
        ),
        out_specs=P(None, ("band", "ma"), None, None),
        check_vma=False,
    )
```

profile of v0, /device:TPU:0, one launch (start us, length us, event | category | flops | bytes accessed | tf_op | source)
XLA Modules:
  0.0 116.5 jit_solution(8038480277856101105)
XLA Ops:
  0.0 0.0 copy-start
  0.0 0.0 copy-start.4
  0.0 35.4 %cosine_convert_fusion = (bf16[16384,128]{1,0:T(8,128)(2,1)}, bf16[16384,128]{1,0:T(8,128)(2,1)}) fusion(s32[128]{0:T(128)} %param.10), kind=kLoop, calls=%fused_computation.15 | loop fusion | flops 33554432 | bytes 8389120 | tf_op jit(solution)/shard_map/convert.2
  35.4 0.0 copy-done.4
  35.4 13.1 %reshape.236 = bf16[256,16384]{1,0:T(8,128)(2,1)} reshape(bf16[64,2,2,16384]{3,2,1,0:T(2,128)(2,1)} %param.7) | data formatting | bytes 16777216 | tf_op jit(solution)/shard_map/reshape | solution.py:39
  48.6 0.0 copy-start.5
  48.6 0.0 copy-start.3
  48.6 0.0 copy-start.6
  48.6 8.3 %fusion.25 = f32[256,256]{0,1:T(8,128)S(1)} fusion(bf16[256,16384]{1,0:T(8,128)(2,1)} %reshape.236, bf16[16384,128]{1,0:T(8,128)(2,1)} %get-tuple-element.22, bf16[16384,128]{1,0:T(8,128)(2,1)} %get-tuple-element.21), kind=kOutput, calls=%fused_computation.38 | convolution fusion | flops 2164260864 | bytes 17039360 | tf_op jit(solution)/shard_map/dot_general | solution.py:38
  56.8 0.1 copy.27
  57.0 0.1 reshape.237
  57.1 0.2 fusion.53
  57.3 0.0 copy-done.5
  57.4 0.1 fusion.42
  57.5 0.1 multiply_convert_fusion.1
  57.6 0.8 copy.30
  58.3 7.3 %all-to-all-start = ((bf16[128,2,256]{2,1,0:T(2,128)(2,1)}), bf16[128,2,256]{2,1,0:T(2,128)(2,1)S(1)}, u32[]{:S(2)}, u32[]{:S(2)}) async-start(bf16[128,2,256]{2,1,0:T(2,128)(2,1)} %copy.30), calls=%async_computation | async-start | bytes 262144 | tf_op jit(solution)/shard_map/all_to_all | solution.py:63
  65.7 0.1 dynamic_slice.3
  65.8 0.0 copy-done.3
  65.8 0.1 fusion.38
  65.9 0.0 copy-done.6
  65.9 0.1 fusion.40
  66.1 0.1 copy.36
  66.2 0.1 copy.37
  66.3 7.2 %all-to-all-done = bf16[128,2,256]{2,1,0:T(2,128)(2,1)S(1)} async-done(((bf16[128,2,256]{2,1,0:T(2,128)(2,1)}), bf16[128,2,256]{2,1,0:T(2,128)(2,1)S(1)}, u32[]{:S(2)}, u32[]{:S(2)}) %all-to-all-start) | async-done | bytes 131104 | tf_op jit(solution)/shard_map/all_to_all | solution.py:63
  73.5 0.1 copy.31
  73.6 0.1 all_to_all.27
  73.6 0.0 copy-done
  73.7 1.8 %convolution_bitcast_fusion = f32[4,3072,256]{1,2,0:T(8,128)S(1)} fusion(bf16[4,64,256]{2,1,0:T(8,128)(2,1)S(1)} %all_to_all.27, bf16[4,3072,64]{1,2,0:T(8,128)(2,1)S(1)} %copy-done), kind=kOutput, calls=%fused_computation.19 | convolution fusion | flops 402653184 | bytes 14286848 | tf_op jit(solution)/shard_map/mlr,mrc->mlc/dot_general | solution.py:64
  75.5 0.0 copy-start.2
  75.5 5.6 %broadcast_multiply_fusion = (f32[4,3072,128]{1,2,0:T(8,128)}, f32[4,3072,128]{1,2,0:T(8,128)}) fusion(f32[4,3072]{1,0:T(4,128)S(1)} %get-tuple-element.20, f32[4,3072,256]{1,2,0:T(8,128)S(1)} %convolution_bitcast_fusion, f32[4,3072]{1,0:T(4,128)S(1)} %get-tuple-element.19), kind=kLoop, calls=%fused_computation.30 | loop fusion | flops 6291456 | bytes 25264128 | tf_op jit(solution)/shard_map/mul | solution.py:67
  81.1 0.0 copy-done.2
  81.1 6.9 %fusion.28 = f32[4,64,256]{2,1,0:T(8,128)S(1)} fusion(bf16[4,3072,64]{1,2,0:T(8,128)(2,1)S(1)} %copy-done.2, f32[4,3072,128]{1,2,0:T(8,128)} %get-tuple-element.5, f32[4,3072,128]{1,2,0:T(8,128)} %get-tuple-element.6), kind=kOutput, calls=%fused_computation.39 | convolution fusion | flops 1211105280 | bytes 14417920 | tf_op jit(solution)/shard_map/mlq,mlc->mqc/dot_general | solution.py:68
  88.0 0.9 copy.33
  88.9 2.8 %all-to-all-start.1 = ((f32[4,64,256]{2,0,1:T(4,128)}), f32[4,64,256]{2,0,1:T(4,128)S(1)}, u32[]{:S(2)}, u32[]{:S(2)}) async-start(f32[4,64,256]{2,0,1:T(4,128)} %copy.33), calls=%async_computation.1 | async-start | bytes 524288 | tf_op jit(solution)/shard_map/all_to_all | solution.py:75
  91.7 9.8 %fusion.31 = (f32[128,4096]{1,0:T(8,128)}, f32[128,4096]{1,0:T(8,128)}) fusion(s32[128]{0:T(128)S(1)} %copy-done.4), kind=kLoop, calls=%fused_computation.40 | loop fusion | flops 7864320 | bytes 4194816 | tf_op jit(solution)/shard_map/cos | solution.py:90
  101.4 0.5 all-to-all-done.1
  101.9 0.1 copy.56
  102.1 0.5 reshape.238
  102.5 0.4 fusion.52
  102.9 0.7 multiply_subtract_fusion
  103.7 0.3 maximum_bitcast_fusion
  103.9 0.4 copy.38
  104.3 0.0 copy-start.1
  104.3 6.3 %convolution_multiply_fusion = f32[256,4096]{1,0:T(8,128)} fusion(f32[128,4096]{1,0:T(8,128)} %get-tuple-element.24, f32[128,4096]{1,0:T(8,128)} %get-tuple-element.23, f32[32,8,2,128]{3,2,1,0:T(2,128)S(1)} %bitcast.31), kind=kOutput, calls=%fused_computation.23 | convolution fusion | flops 1612709888 | bytes 8650752 | tf_op jit(solution)/shard_map/dot_general | solution.py:91
  110.6 5.8 %reshape.240 = f32[64,2,2,4096]{3,2,1,0:T(2,128)} reshape(f32[256,4096]{1,0:T(8,128)} %convolution_multiply_fusion) | data formatting | bytes 8388608 | tf_op jit(solution)/shard_map/reshape | solution.py:95
  116.5 0.0 copy-done.1
  (5 shorter events, 0.0 us)
Async XLA Ops:
  0.0 73.6 %copy-start = (bf16[4,3072,64]{1,2,0:T(8,128)(2,1)S(1)}, bf16[4,3072,64]{1,2,0:T(8,128)(2,1)}, u32[]{:S(2)}) copy-start(bf16[4,3072,64]{1,2,0:T(8,128)(2,1)} %param.11) | copy-start | bytes 4718596
  0.0 35.4 %copy-start.4 = (s32[128]{0:T(128)S(1)}, s32[128]{0:T(128)}, u32[]{:S(2)}) copy-start(s32[128]{0:T(128)} %param.10) | copy-start | bytes 1540
  48.6 8.8 %copy-start.5 = (s32[2]{0:T(128)S(1)}, s32[2]{0:T(128)}, u32[]{:S(2)}) copy-start(s32[2]{0:T(128)} %param.8) | copy-start | bytes 28
  48.6 17.2 %copy-start.3 = (f32[3072]{0:T(1024)S(1)}, f32[3072]{0:T(1024)}, u32[]{:S(2)}) copy-start(f32[3072]{0:T(1024)} %param.13) | copy-start | bytes 36868
  48.6 17.4 %copy-start.6 = (s32[2]{0:T(128)S(1)}, s32[2]{0:T(128)}, u32[]{:S(2)}) copy-start(s32[2]{0:T(128)} %param.9) | copy-start | bytes 28
  58.3 15.1 %all-to-all-start = ((bf16[128,2,256]{2,1,0:T(2,128)(2,1)}), bf16[128,2,256]{2,1,0:T(2,128)(2,1)S(1)}, u32[]{:S(2)}, u32[]{:S(2)}) async-start(bf16[128,2,256]{2,1,0:T(2,128)(2,1)} %copy.30), calls=%async_computation | async-start | bytes 262144 | tf_op jit(solution)/shard_map/all_to_all | solution.py:63
  75.5 5.6 %copy-start.2 = (bf16[4,3072,64]{1,2,0:T(8,128)(2,1)S(1)}, bf16[4,3072,64]{1,2,0:T(8,128)(2,1)}, u32[]{:S(2)}) copy-start(bf16[4,3072,64]{1,2,0:T(8,128)(2,1)} %param.12) | copy-start | bytes 4718596
  88.9 13.0 %all-to-all-start.1 = ((f32[4,64,256]{2,0,1:T(4,128)}), f32[4,64,256]{2,0,1:T(4,128)S(1)}, u32[]{:S(2)}, u32[]{:S(2)}) async-start(f32[4,64,256]{2,0,1:T(4,128)} %copy.33), calls=%async_computation.1 | async-start | bytes 524288 | tf_op jit(solution)/shard_map/all_to_all | solution.py:75
  104.3 12.2 %copy-start.1 = (bf16[4,3072,64]{1,2,0:T(8,128)(2,1)S(1)}, bf16[4,3072,64]{1,2,0:T(8,128)(2,1)}, u32[]{:S(2)}) copy-start(bf16[4,3072,64]{1,2,0:T(8,128)(2,1)} %param.11) | copy-start | bytes 4718596
where the time goes:
time: 117 us; the launch traced here: 116 us
  other arithmetic  52.2 us (45%)
  matrix products  23.4 us (20%)
  local copies, waits for them, and re-layouts  22.9 us (20%)
  starting transfers between devices  10.1 us (9%)
  waiting for transfers between devices  7.68 us (7%)
    another operation x2, other arithmetic  35.5 us
    reshape x1, local copies, waits for them, and re-layouts, per_device(): sky_maps.reshape(-1, NPIX_HI)  13.1 us
    cos x1, other arithmetic, per_device(): jnp.cos(angles_lo)  9.79 us
    dot_general x1, matrix products, per_device(): jnp.dot(sky_maps.reshape(-1, NPIX_HI), forward_table, preferred_element_t...  8.27 us
    all_to_all x1, starting transfers between devices, per_device(): lax.all_to_all(outgoing, ('band', 'ma'), split_axis=0, concat_axis=1, til...  7.32 us
    all_to_all x1, waiting for transfers between devices, per_device(): lax.all_to_all(outgoing, ('band', 'ma'), split_axis=0, concat_axis=1, til...  7.21 us
    dot_general x1, matrix products, per_device(): jnp.einsum('mlq,mlc->mqc', legendre_lo, paired, precision=THREE_PASS, pre...  6.94 us
    dot_general x1, matrix products, per_device(): jnp.dot(spectra, inverse_table, precision=THREE_PASS, preferred_element_t...  6.33 us
  transfers between devices with their start and end apart: 2, of which 2 were waited for; matrix products, arithmetic and copies ran while one was open for 9% of the time, Pallas kernels for 0%

commit v1 on v0

v1 whole, which is shorter than its diff:
```python
import functools
import math

import jax
import jax.numpy as jnp
from jax import lax
from jax.experimental import pallas as pl
from jax.experimental.pallas import tpu as pltpu
from jax.sharding import PartitionSpec as P

NSIDE_HI = 4096
NSIDE_LO = 1024
NPIX_HI = 16384
NPIX_LO = 4096

LANES = 128
HEMIS = 2
BF16_ROWS = 16
F32_ROWS = 8
F32 = jnp.float32
BF16 = jnp.bfloat16


def unit_circle(steps, length):
    quarter = length // 4
    quadrant = (steps + quarter // 2) // quarter
    rest = steps - quadrant * quarter
    angle = rest.astype(F32) * (2.0 * math.pi / length)
    square = angle * angle
    sine = square * (1.0 / 362880.0) - 1.0 / 5040.0
    sine = square * sine + 1.0 / 120.0
    sine = square * sine - 1.0 / 6.0
    sine = angle + angle * (square * sine)
    cosine = square * (-1.0 / 3628800.0) + 1.0 / 40320.0
    cosine = square * cosine - 1.0 / 720.0
    cosine = square * cosine + 1.0 / 24.0
    cosine = square * cosine - 0.5
    cosine = 1.0 + square * cosine
    odd = (quadrant & 1) == 1
    big = jnp.where(odd, sine, cosine)
    small = jnp.where(odd, cosine, sine)
    cos_out = jnp.where(((quadrant + 1) & 2) == 2, -big, big)
    sin_out = jnp.where((quadrant & 2) == 2, -small, small)
    return cos_out, sin_out


def iota(shape, dim):
    return lax.broadcasted_iota(jnp.int32, shape, dim)


def split(value):
    high = value.astype(BF16)
    return high, (value - high.astype(F32)).astype(BF16)


def analyse_kernel(hi_ref, orders_ref, sky_ref, out_ref, sky, table, sums, sems):
    chunks, rows_mp, blocks = sky.shape[:3]
    pairs = hi_ref.shape[0]
    orders = orders_ref[...]
    count = orders.shape[1]
    maps_here = rows_mp // pairs
    inner = BF16_ROWS // HEMIS
    copies = [
        pltpu.make_async_copy(
            sky_ref.at[pl.ds(c * rows_mp, rows_mp)], sky.at[c], sems.at[c]
        )
        for c in range(chunks)
    ]
    for copy in copies:
        copy.start()

    cos_l, sin_l = unit_circle(orders * iota((LANES, count), 0) & (NPIX_HI - 1), NPIX_HI)
    stride = inner * LANES
    cos_a, sin_a = unit_circle(
        orders * (stride * iota((blocks, count), 0)) & (NPIX_HI - 1), NPIX_HI
    )
    for a in range(blocks):
        ca, sa = cos_a[a : a + 1], sin_a[a : a + 1]
        table[a * LANES : (a + 1) * LANES, :count] = (ca * cos_l - sa * sin_l).astype(BF16)
        table[a * LANES : (a + 1) * LANES, count:] = (sa * cos_l + ca * sin_l).astype(BF16)

    scale = 1.0 / math.sqrt(NPIX_HI)
    phases = []
    for p in range(pairs):
        offset = (hi_ref[p] - NSIDE_HI + 1) & 1
        step = 2 * LANES * (iota((BF16_ROWS, count), 0) // HEMIS) + offset
        phases.append(unit_circle(orders * step & (2 * NPIX_HI - 1), 2 * NPIX_HI))
    cos_p = jnp.stack([c * scale for c, _ in phases])[None]
    sin_p = jnp.stack([s * scale for _, s in phases])[None]

    def reduce_blocks(value):
        value = value[:, :, :F32_ROWS] + value[:, :, F32_ROWS:]
        value = value.reshape(rows_mp, F32_ROWS, count)
        value = value + pltpu.roll(value, 4, 1)
        return value + pltpu.roll(value, 2, 1)

    for c in range(chunks):
        copies[c].wait()
        rows = jnp.concatenate(
            [sky[c, :, a].reshape(rows_mp * BF16_ROWS, LANES) for a in range(blocks)], axis=1
        )
        raw = jnp.dot(rows, table[...], preferred_element_type=F32)
        raw = raw.reshape(maps_here, pairs, BF16_ROWS, 2 * count)
        raw_c, raw_s = raw[..., :count], raw[..., count:]
        real = reduce_blocks(raw_c * cos_p - raw_s * sin_p)
        imag = reduce_blocks(-(raw_c * sin_p + raw_s * cos_p))
        for i in range(maps_here):
            for p in range(pairs):
                for h in range(HEMIS):
                    at = pl.ds(c * maps_here + i, 1)
                    sums[p, h, 0, at, :] = real[i * pairs + p, h : h + 1]
                    sums[p, h, 1, at, :] = imag[i * pairs + p, h : h + 1]
    out_ref[...] = sums[...].astype(BF16)


def harmonic_kernel(own_ref, coeff_ref, hi_ref, lo_ref, beam_ref, out_ref):
    order = own_ref[pl.program_id(0)]
    degrees = iota(beam_ref.shape, 1)
    sign = (1 - 2 * ((degrees + order) & 1)).astype(F32)
    weight = jnp.where(degrees >= order, beam_ref[...], 0.0)
    half = coeff_ref.shape[2] // 2
    coeff = jnp.concatenate([coeff_ref[0, :, :half], coeff_ref[0, :, half:]], axis=0)

    def both(table):
        flipped = (table.astype(F32) * sign).astype(BF16)
        return jnp.concatenate([table, flipped], axis=0)

    alm = lax.dot_general(
        coeff, both(hi_ref[0]), (((0,), (0,)), ((), ())), preferred_element_type=F32
    )
    high, low = split(alm * weight)
    table = both(lo_ref[0])
    dims = (((1,), (1,)), ((), ()))
    total = lax.dot_general(table, high, dims, preferred_element_type=F32)
    total += lax.dot_general(table, low, dims, preferred_element_type=F32)
    out_ref[0] = total.astype(out_ref.dtype)


def synthesise_kernel(
    lo_ref, orders_ref, column_ref, coeff_ref, out_ref, table_hi, table_lo, spectra, phase
):
    maps_here, pairs, blocks = out_ref.shape[:3]
    count = orders_ref.shape[1]
    map_count = spectra.shape[3]

    @pl.when(pl.program_id(0) == 0)
    def _():
        column = column_ref[...]
        orders = orders_ref[...]
        for a in range(blocks):
            pixel = a * (F32_ROWS // HEMIS * LANES) + iota((count, LANES), 1)
            cosine, sine = unit_circle(column * pixel & (NPIX_LO - 1), NPIX_LO)
            lanes = slice(a * LANES, (a + 1) * LANES)
            table_hi[:count, lanes], table_lo[:count, lanes] = split(cosine)
            table_hi[count:, lanes], table_lo[count:, lanes] = split(-sine)
        scale = math.sqrt(2.0 / count)
        for p in range(pairs):
            offset = (lo_ref[p] - NSIDE_LO + 1) & 1
            step = 2 * LANES * (iota((F32_ROWS, count), 0) // HEMIS) + offset
            cosine, sine = unit_circle(orders * step & (2 * NPIX_LO - 1), 2 * NPIX_LO)
            phase[p, 0] = cosine * scale
            phase[p, 1] = sine * scale
            turned = coeff_ref[p].astype(F32).T
            spectra[p] = turned.reshape(HEMIS, 2, map_count, count)

    rows = pl.ds(pl.multiple_of(pl.program_id(0) * maps_here, maps_here), maps_here)
    south = (iota((1, F32_ROWS, count), 1) & 1) == 1
    parts = []
    for p in range(pairs):
        def spread(c):
            north_rows = spectra[p, 0, c, rows, :]
            south_rows = spectra[p, 1, c, rows, :]
            return jnp.where(south, south_rows[:, None, :], north_rows[:, None, :])

        real, imag = spread(0), spread(1)
        cosine, sine = phase[p, 0][None], phase[p, 1][None]
        turned = jnp.concatenate(
            [real * cosine - imag * sine, imag * cosine + real * sine], axis=2
        )
        parts.append(turned.reshape(maps_here * F32_ROWS, 2 * count))
    high, low = split(jnp.concatenate(parts, axis=0))
    pixels = jnp.dot(high, table_hi[...], preferred_element_type=F32)
    pixels += jnp.dot(low, table_hi[...], preferred_element_type=F32)
    pixels += jnp.dot(high, table_lo[...], preferred_element_type=F32)
    pixels = pixels.reshape(pairs, maps_here, F32_ROWS, blocks * LANES)
    for p in range(pairs):
        for a in range(blocks):
            out_ref[:, p, a] = pixels[p, :, :, a * LANES : (a + 1) * LANES]


def vmem():
    return pl.BlockSpec(memory_space=pltpu.VMEM)


def smem():
    return pl.BlockSpec(memory_space=pltpu.SMEM)


def per_device(
    sky_maps, hi_cycles, lo_cycles, azimuth_orders, legendre_hi, legendre_lo, beam_weights
):
    axes = ("band", "ma")
    map_count, pairs = sky_maps.shape[:2]
    count = azimuth_orders.shape[0]
    owned, degree_count, pair_total = legendre_hi.shape
    low_total = legendre_lo.shape[2]
    order_row = azimuth_orders.reshape(1, count)
    order_column = azimuth_orders.reshape(count, 1)
    cols = HEMIS * 2 * map_count

    inner = BF16_ROWS // HEMIS
    blocks = NPIX_HI // (inner * LANES)
    sky = sky_maps.reshape(map_count, pairs, HEMIS, blocks, inner, LANES)
    sky = sky.transpose(0, 1, 3, 4, 2, 5)
    sky = sky.reshape(map_count * pairs, blocks, BF16_ROWS, LANES)
    rows_mp = 8 * pairs
    chunks = map_count * pairs // rows_mp
    coeffs = pl.pallas_call(
        analyse_kernel,
        out_shape=jax.ShapeDtypeStruct((pairs, HEMIS, 2, map_count, count), BF16),
        in_specs=[smem(), vmem(), pl.BlockSpec(memory_space=pl.ANY)],
        out_specs=vmem(),
        scratch_shapes=[
            pltpu.VMEM((chunks, rows_mp, blocks, BF16_ROWS, LANES), BF16),
            pltpu.VMEM((blocks * LANES, 2 * count), BF16),
            pltpu.VMEM((pairs, HEMIS, 2, map_count, count), F32),
            pltpu.SemaphoreType.DMA((chunks,)),
        ],
        compiler_params=pltpu.CompilerParams(vmem_limit_bytes=32 * 2**20),
        name="analyse",
    )(hi_cycles, order_row, sky)
    outgoing = coeffs.reshape(pairs, cols, count).transpose(2, 0, 1)
    received = lax.all_to_all(outgoing, axes, split_axis=0, concat_axis=1, tiled=True)

    own = lax.dynamic_slice_in_dim(azimuth_orders, lax.axis_index(axes) * owned, owned)
    harmonic = pl.pallas_call(
        harmonic_kernel,
        grid=(owned,),
        out_shape=jax.ShapeDtypeStruct((owned, HEMIS * low_total, 2 * map_count), BF16),
        in_specs=[
            smem(),
            pl.BlockSpec((1, pair_total, cols), lambda g: (g, 0, 0)),
            pl.BlockSpec((1, pair_total, degree_count), lambda g: (g, 0, 0)),
            pl.BlockSpec((1, low_total, degree_count), lambda g: (g, 0, 0)),
            pl.BlockSpec((1, degree_count), lambda g: (0, 0)),
        ],
        out_specs=pl.BlockSpec((1, HEMIS * low_total, 2 * map_count), lambda g: (g, 0, 0)),
        compiler_params=pltpu.CompilerParams(vmem_limit_bytes=32 * 2**20),
        name="harmonic",
    )(
        own,
        received,
        legendre_hi.transpose(0, 2, 1),
        legendre_lo.transpose(0, 2, 1),
        beam_weights.reshape(1, degree_count),
    )
    synthesised = harmonic.reshape(owned, HEMIS, low_total, 2 * map_count)
    synthesised = synthesised.transpose(0, 2, 1, 3).reshape(owned, low_total, cols)
    returned = lax.all_to_all(synthesised, axes, split_axis=1, concat_axis=0, tiled=True)

    blocks_lo = NPIX_LO // (F32_ROWS // HEMIS * LANES)
    maps_here = 16
    pixels = pl.pallas_call(
        synthesise_kernel,
        grid=(map_count // maps_here,),
        out_shape=jax.ShapeDtypeStruct((map_count, pairs, blocks_lo, F32_ROWS, LANES), F32),
        in_specs=[
            smem(),
            pl.BlockSpec((1, count), lambda i: (0, 0)),
            pl.BlockSpec((count, 1), lambda i: (0, 0)),
            pl.BlockSpec((pairs, count, cols), lambda i: (0, 0, 0)),
        ],
        out_specs=pl.BlockSpec(
            (maps_here, pairs, blocks_lo, F32_ROWS, LANES), lambda i: (i, 0, 0, 0, 0)
        ),
        scratch_shapes=[
            pltpu.VMEM((2 * count, blocks_lo * LANES), BF16),
            pltpu.VMEM((2 * count, blocks_lo * LANES), BF16),
            pltpu.VMEM((pairs, HEMIS, 2, map_count, count), F32),
            pltpu.VMEM((pairs, 2, F32_ROWS, count), F32),
        ],
        compiler_params=pltpu.CompilerParams(vmem_limit_bytes=32 * 2**20),
        name="synthesise",
    )(lo_cycles, order_row, order_column, returned.transpose(1, 0, 2))
    pixels = pixels.reshape(map_count, pairs, blocks_lo, F32_ROWS // HEMIS, HEMIS, LANES)
    pixels = pixels.transpose(0, 1, 4, 2, 3, 5)
    return pixels.reshape(map_count, pairs, HEMIS, NPIX_LO)


def solution(mesh):
    spread = ("band", "ma")
    return jax.shard_map(
        per_device,
        mesh=mesh,
        in_specs=(
            P(None, spread, None, None),
            P(spread),
            P(spread),
            P(),
            P(spread, None, None),
            P(spread, None, None),
            P(),
        ),
        out_specs=P(None, spread, None, None),
        check_vma=False,
    )
```

time: 117 us -> 51 us (0.44)
  other arithmetic: 52.2 us -> 0 us
  matrix products: 23.4 us -> 0 us
  Pallas kernels: 0 us -> 18.4 us
  local copies, waits for them, and re-layouts: 22.9 us -> 6.91 us
  waiting for transfers between devices: 7.68 us -> 15.4 us
    another operation x3 -> x0, other arithmetic: 35.5 us -> none
    dot_general x4 -> x0, matrix products: 23.4 us -> none  [the longest x1 8.27 us: per_device(): jnp.dot(sky_maps.reshape(-1, NPIX_HI), forward_table, preferred_element_t...]
    pallas_call x0 -> x3, Pallas kernels: none -> 18.4 us  [the longest x1 7.24 us: per_device(): pl.pallas_call(analyse_kernel, out_shape=jax.ShapeDtypeStruct((pairs, HEM...]
    reshape x4 -> x5, local copies, waits for them, and re-layouts: 19.5 us -> 1.89 us  [the longest x2 0.85 us: per_device(): synthesised.transpose(0, 2, 1, 3).reshape(owned, low_total, cols)]
    cos x3 -> x0, other arithmetic: 10 us -> none  [the longest x1 9.79 us: per_device(): jnp.cos(angles_lo)]
    all_to_all x2, waiting for transfers between devices: 7.68 us -> 15.4 us  [the longest x1 7.71 us: per_device(): lax.all_to_all(outgoing, axes, split_axis=0, concat_axis=1, tiled=True)]
    mul x3 -> x0, other arithmetic: 5.59 us -> none  [the longest x1 5.57 us: per_device(): paired = jnp.concatenate([weighted, signs_lm[..., None] * weighted], axis=2)]
    unnamed x14 -> x16, local copies, waits for them, and re-layouts: 0.03 us -> 4.71 us
  transfers between devices with their start and end apart: 2 -> 2, of which waited for: 2 -> 2; matrix products, arithmetic and copies ran while one was open for 9% -> 0% of each run, Pallas kernels for 0% -> 0%
where the time goes in v1:
time: 51 us; the launch traced here: 50.7 us
  Pallas kernels  18.4 us (36%)
  waiting for transfers between devices  15.4 us (30%)
  starting transfers between devices  9.9 us (19%)
  local copies, waits for them, and re-layouts  6.91 us (14%)
    all_to_all x1, waiting for transfers between devices, per_device(): lax.all_to_all(outgoing, axes, split_axis=0, concat_axis=1, tiled=True)  7.71 us
    all_to_all x1, waiting for transfers between devices, per_device(): lax.all_to_all(synthesised, axes, split_axis=1, concat_axis=0, tiled=True)  7.69 us
    all_to_all x1, starting transfers between devices, per_device(): lax.all_to_all(outgoing, axes, split_axis=0, concat_axis=1, tiled=True)  7.33 us
    pallas_call x1, Pallas kernels, per_device(): pl.pallas_call(analyse_kernel, out_shape=jax.ShapeDtypeStruct((pairs, HEM...  7.24 us
    pallas_call x1, Pallas kernels, per_device(): pl.pallas_call(synthesise_kernel, grid=(map_count // maps_here,), out_sha...  5.86 us
    pallas_call x1, Pallas kernels, per_device(): pl.pallas_call(harmonic_kernel, grid=(owned,), out_shape=jax.ShapeDtypeSt...  5.28 us
    unnamed x16, local copies, waits for them, and re-layouts  4.71 us
    all_to_all x1, starting transfers between devices, per_device(): lax.all_to_all(synthesised, axes, split_axis=1, concat_axis=0, tiled=True)  2.58 us
  transfers between devices with their start and end apart: 2, of which 2 were waited for; matrix products, arithmetic and copies ran while one was open for 0% of the time, Pallas kernels for 0%

profile of v1, /device:TPU:0, one launch (start us, length us, event | category | flops | bytes accessed | tf_op | source)
XLA Modules:
  0.0 50.7 jit_solution(8449811926877184142)
XLA Ops:
  0.0 0.0 copy-start
  0.0 3.4 %copy-done = bf16[64,2,2,16384]{3,2,1,0:T(2,128)(2,1)S(1)} copy-done((bf16[64,2,2,16384]{3,2,1,0:T(2,128)(2,1)S(1)}, bf16[64,2,2,16384]{3,2,1,0:T(2,128)(2,1)}, u32[]{:S(2)}) %copy-start) | copy-done | bytes 8388632
  3.4 0.0 copy-start.4
  3.4 0.7 %copy-done.4 = s32[128]{0:T(128)S(1)} copy-done((s32[128]{0:T(128)S(1)}, s32[128]{0:T(128)}, u32[]{:S(2)}) %copy-start.4) | copy-done | bytes 536
  4.0 0.0 copy-start.6
  4.0 0.7 %copy-done.6 = s32[2]{0:T(128)S(1)} copy-done((s32[2]{0:T(128)S(1)}, s32[2]{0:T(128)}, u32[]{:S(2)}) %copy-start.6) | copy-done | bytes 32
  4.7 0.0 copy-start.5
  4.7 0.0 copy-start.1
  4.7 0.0 copy-start.2
  4.7 0.0 copy-start.3
  4.7 7.2 %analyse.1 = bf16[2,2,2,64,128]{4,3,2,1,0:T(8,128)(2,1)S(1)} custom-call(s32[2]{0:T(128)S(1)} %copy-done.6, s32[1,128]{1,0:T(1,128)S(1)} %bitcast.37, bf16[128,16,16,128]{3,2,1,0:T(8,128)(2,1)S(1)} %bitcast.30), custom_call_target="tpu_custom_call" | custom-call | tf_op jit(solution)/shard_map/analyse/pallas_call | solution.py:218
  12.0 0.0 copy-start.7
  12.0 0.8 %copy.20 = bf16[2,256,128]{1,0,2:T(2,128)(2,1)} copy(bf16[2,256,128]{2,1,0:T(8,128)(2,1)S(1)} %bitcast.33) | data formatting | bytes 262144 | tf_op jit(solution)/shard_map/reshape | solution.py:232
  12.8 7.3 %all-to-all-start = ((bf16[128,2,256]{2,1,0:T(2,128)(2,1)}), bf16[128,2,256]{2,1,0:T(2,128)(2,1)S(1)}, u32[]{:S(2)}, u32[]{:S(2)}) async-start(bf16[128,2,256]{2,1,0:T(2,128)(2,1)} %bitcast.6), calls=%async_computation | async-start | bytes 262144 | tf_op jit(solution)/shard_map/all_to_all | solution.py:233
  20.1 0.0 copy-done.5
  20.1 0.1 dynamic_slice.3.own_ref
  20.2 7.7 %all-to-all-done = bf16[128,2,256]{2,1,0:T(2,128)(2,1)S(1)} async-done(((bf16[128,2,256]{2,1,0:T(2,128)(2,1)}), bf16[128,2,256]{2,1,0:T(2,128)(2,1)S(1)}, u32[]{:S(2)}, u32[]{:S(2)}) %all-to-all-start) | async-done | bytes 131104 | tf_op jit(solution)/shard_map/all_to_all | solution.py:233
  27.9 0.1 copy.21
  28.0 0.1 all_to_all.29.coeff_ref
  28.1 0.0 copy-done.1
  28.1 0.0 copy-done.2
  28.1 0.0 copy-done.3
  28.1 5.3 %harmonic.1 = bf16[4,128,128]{2,1,0:T(8,128)(2,1)S(1)} custom-call(s32[4]{0:T(128)S(1)} %dynamic_slice.3.own_ref, bf16[4,64,256]{2,1,0:T(8,128)(2,1)S(1)} %all_to_all.29.coeff_ref, bf16[4,64,3072]{2,1,0:T(8,128)(2,1)S(1)} %bitcast.31, bf16[4,64,3072]{2,1,0:T(8,128)(2,1)S(1)} %bitcast.32, f32[1,3072]{1,0:T(1,128)S(1)} %bitcast.36), custom_call_target="tpu_custom_call" | custom-call | tf_op jit(solution)/shard_map/harmonic/pallas_call | solution.py:236
  33.4 0.1 copy.28
  33.5 0.1 reshape.37
  33.6 0.8 %copy.23 = bf16[4,64,256]{2,0,1:T(4,128)(2,1)} copy(bf16[4,64,256]{2,1,0:T(8,128)(2,1)S(1)} %reshape.37) | data formatting | bytes 262144 | tf_op jit(solution)/shard_map/reshape | solution.py:258
  34.4 2.6 %all-to-all-start.1 = ((bf16[4,64,256]{2,0,1:T(4,128)(2,1)}), bf16[4,64,256]{2,0,1:T(4,128)(2,1)S(1)}, u32[]{:S(2)}, u32[]{:S(2)}) async-start(bf16[4,64,256]{2,0,1:T(4,128)(2,1)} %copy.23), calls=%async_computation.1 | async-start | bytes 262144 | tf_op jit(solution)/shard_map/all_to_all | solution.py:259
  37.0 0.1 copy.25.column_ref
  37.1 7.7 %all-to-all-done.1 = bf16[4,64,256]{2,0,1:T(4,128)(2,1)S(1)} async-done(((bf16[4,64,256]{2,0,1:T(4,128)(2,1)}), bf16[4,64,256]{2,0,1:T(4,128)(2,1)S(1)}, u32[]{:S(2)}, u32[]{:S(2)}) %all-to-all-start.1) | async-done | bytes 131104 | tf_op jit(solution)/shard_map/all_to_all | solution.py:259
  44.9 0.0 copy-done.7
  44.9 5.9 %synthesise.1 = f32[64,2,8,8,128]{4,3,2,1,0:T(8,128)} custom-call(s32[2]{0:T(128)S(1)} %copy-done.7, s32[1,128]{1,0:T(1,128)S(1)} %bitcast.39, s32[128,1]{1,0:T(8,128)S(1)} %copy.25.column_ref, bf16[2,128,256]{2,1,0:T(8,128)(2,1)S(1)} %bitcast.35), custom_call_target="tpu_custom_call" | custom-call | tf_op jit(solution)/shard_map/synthesise/pallas_call | solution.py:263
  (2 shorter events, 0.1 us)
Async XLA Ops:
  0.0 3.4 %copy-start = (bf16[64,2,2,16384]{3,2,1,0:T(2,128)(2,1)S(1)}, bf16[64,2,2,16384]{3,2,1,0:T(2,128)(2,1)}, u32[]{:S(2)}) copy-start(bf16[64,2,2,16384]{3,2,1,0:T(2,128)(2,1)} %param.7) | copy-start | bytes 25165828
  3.4 0.7 %copy-start.4 = (s32[128]{0:T(128)S(1)}, s32[128]{0:T(128)}, u32[]{:S(2)}) copy-start(s32[128]{0:T(128)} %param.10) | copy-start | bytes 1540
  4.0 0.7 %copy-start.6 = (s32[2]{0:T(128)S(1)}, s32[2]{0:T(128)}, u32[]{:S(2)}) copy-start(s32[2]{0:T(128)} %hi_ref.1) | copy-start | bytes 28
  4.7 15.4 %copy-start.5 = (s32[128]{0:T(128)S(1)}, s32[128]{0:T(128)}, u32[]{:S(2)}) copy-start(s32[128]{0:T(128)} %param.10) | copy-start | bytes 1540
  4.7 23.4 %copy-start.1 = (bf16[4,3072,64]{1,2,0:T(8,128)(2,1)S(1)}, bf16[4,3072,64]{1,2,0:T(8,128)(2,1)}, u32[]{:S(2)}) copy-start(bf16[4,3072,64]{1,2,0:T(8,128)(2,1)} %param.11) | copy-start | bytes 4718596
  4.7 23.4 %copy-start.2 = (bf16[4,3072,64]{1,2,0:T(8,128)(2,1)S(1)}, bf16[4,3072,64]{1,2,0:T(8,128)(2,1)}, u32[]{:S(2)}) copy-start(bf16[4,3072,64]{1,2,0:T(8,128)(2,1)} %param.12) | copy-start | bytes 4718596
  4.7 23.4 %copy-start.3 = (f32[3072]{0:T(1024)S(1)}, f32[3072]{0:T(1024)}, u32[]{:S(2)}) copy-start(f32[3072]{0:T(1024)} %param.13) | copy-start | bytes 36868
  12.0 32.9 %copy-start.7 = (s32[2]{0:T(128)S(1)}, s32[2]{0:T(128)}, u32[]{:S(2)}) copy-start(s32[2]{0:T(128)} %lo_ref.1) | copy-start | bytes 28
  12.8 15.1 %all-to-all-start = ((bf16[128,2,256]{2,1,0:T(2,128)(2,1)}), bf16[128,2,256]{2,1,0:T(2,128)(2,1)S(1)}, u32[]{:S(2)}, u32[]{:S(2)}) async-start(bf16[128,2,256]{2,1,0:T(2,128)(2,1)} %bitcast.6), calls=%async_computation | async-start | bytes 262144 | tf_op jit(solution)/shard_map/all_to_all | solution.py:233
  34.4 10.4 %all-to-all-start.1 = ((bf16[4,64,256]{2,0,1:T(4,128)(2,1)}), bf16[4,64,256]{2,0,1:T(4,128)(2,1)S(1)}, u32[]{:S(2)}, u32[]{:S(2)}) async-start(bf16[4,64,256]{2,0,1:T(4,128)(2,1)} %copy.23), calls=%async_computation.1 | async-start | bytes 262144 | tf_op jit(solution)/shard_map/all_to_all | solution.py:259

commit v2 on v1

v2 whole, which is shorter than its diff:
```python
import functools
import math

import jax
import jax.numpy as jnp
from jax import lax
from jax.experimental import pallas as pl
from jax.experimental.pallas import tpu as pltpu
from jax.sharding import PartitionSpec as P

NSIDE_HI = 4096
NSIDE_LO = 1024
NPIX_HI = 16384
NPIX_LO = 4096

LANES = 128
HEMIS = 2
BF16_ROWS = 16
F32_ROWS = 8
F32 = jnp.float32
BF16 = jnp.bfloat16


def unit_circle(steps, length):
    quarter = length // 4
    quadrant = (steps + quarter // 2) // quarter
    rest = steps - quadrant * quarter
    angle = rest.astype(F32) * (2.0 * math.pi / length)
    square = angle * angle
    sine = square * (1.0 / 362880.0) - 1.0 / 5040.0
    sine = square * sine + 1.0 / 120.0
    sine = square * sine - 1.0 / 6.0
    sine = angle + angle * (square * sine)
    cosine = square * (-1.0 / 3628800.0) + 1.0 / 40320.0
    cosine = square * cosine - 1.0 / 720.0
    cosine = square * cosine + 1.0 / 24.0
    cosine = square * cosine - 0.5
    cosine = 1.0 + square * cosine
    odd = (quadrant & 1) == 1
    big = jnp.where(odd, sine, cosine)
    small = jnp.where(odd, cosine, sine)
    cos_out = jnp.where(((quadrant + 1) & 2) == 2, -big, big)
    sin_out = jnp.where((quadrant & 2) == 2, -small, small)
    return cos_out, sin_out


def iota(shape, dim):
    return lax.broadcasted_iota(jnp.int32, shape, dim)


def split(value):
    high = value.astype(BF16)
    return high, (value - high.astype(F32)).astype(BF16)


def one_hot(shape, match):
    return jnp.where(match(iota(shape, 0), iota(shape, 1)), 1.0, 0.0).astype(BF16)


def dot_tn(lhs, rhs):
    return lax.dot_general(lhs, rhs, (((0,), (0,)), ((), ())), preferred_element_type=F32)


def dot_nt(lhs, rhs):
    return lax.dot_general(lhs, rhs, (((1,), (1,)), ((), ())), preferred_element_type=F32)


def dot_nn(lhs, rhs):
    return jnp.dot(lhs, rhs, preferred_element_type=F32)


def pair_rows(pairs):
    side = LANES * pairs
    return one_hot((side, side), lambda i, j: i == j % LANES * pairs + j // LANES)


def analyse_kernel(
    spans, hi_hbm, orders_hbm, sky_hbm, out_ref, hi, orders_ref, sky, table, raw_a, raw_b, sums, sems
):
    raws = (raw_a, raw_b)
    blocks = sky.shape[1]
    pairs = hi.shape[0]
    count = orders_ref.shape[1]
    map_count = sky.shape[0] // pairs
    inner = BF16_ROWS // HEMIS
    small = [
        pltpu.make_async_copy(orders_hbm, orders_ref, sems.at[0]),
        pltpu.make_async_copy(hi_hbm, hi, sems.at[1]),
    ]
    copies = []
    for c, (start, size) in enumerate(spans):
        part = pl.ds(start * pairs, size * pairs)
        copies.append(pltpu.make_async_copy(sky_hbm.at[part], sky.at[part], sems.at[2 + c]))
    for copy in small + copies:
        copy.start()

    gather = pair_rows(pairs)
    for copy in small:
        copy.wait()
    orders = orders_ref[...]
    cos_l, sin_l = unit_circle(orders * iota((LANES, count), 0) & (NPIX_HI - 1), NPIX_HI)
    stride = inner * LANES
    cos_a, sin_a = unit_circle(
        orders * (stride * iota((blocks, count), 0)) & (NPIX_HI - 1), NPIX_HI
    )
    scale = 1.0 / math.sqrt(NPIX_HI)
    cos_p, sin_p = [], []
    for p in range(pairs):
        offset = (hi[p] - NSIDE_HI + 1) & 1
        step = 2 * LANES * (iota((BF16_ROWS, count), 0) // HEMIS) + offset
        cosine, sine = unit_circle(orders * step & (2 * NPIX_HI - 1), 2 * NPIX_HI)
        cos_p.append(cosine * scale)
        sin_p.append(sine * scale)
    copies[0].wait()
    for a in range(blocks):
        ca, sa = cos_a[a : a + 1], sin_a[a : a + 1]
        table[a * LANES : (a + 1) * LANES, :count] = (ca * cos_l - sa * sin_l).astype(BF16)
        table[a * LANES : (a + 1) * LANES, count:] = (sa * cos_l + ca * sin_l).astype(BF16)

    def contract(c):
        start, size = spans[c]
        part = slice(start * pairs, (start + size) * pairs)
        rows = jnp.concatenate(
            [sky[part, a].reshape(size * pairs * BF16_ROWS, LANES) for a in range(blocks)], axis=1
        )
        raws[c % 2][: size * pairs * BF16_ROWS] = dot_nn(rows, table[...])

    sub = iota((1, F32_ROWS, count), 1)

    def sum_blocks(value):
        value = value[:, :F32_ROWS] + value[:, F32_ROWS:]
        low, high = value[:4], value[4:]
        first = sub < 4
        value = jnp.where(first, low, high) + pltpu.roll(jnp.where(first, high, low), 4, 1)
        low, high = value[:2], value[2:]
        first = (sub & 2) == 0
        value = jnp.where(first, low + pltpu.roll(low, 6, 1), high + pltpu.roll(high, 2, 1))
        low, high = value[:1], value[1:]
        first = (sub & 1) == 0
        north = jnp.where(first, low, pltpu.roll(high, 1, 1))
        south = jnp.where(first, pltpu.roll(low, 7, 1), high)
        return north[0], south[0]

    def finish(c):
        start, size = spans[c]
        rows = 8 * pairs * BF16_ROWS
        for group in range(size // 8):
            raw = raws[c % 2][group * rows : (group + 1) * rows]
            raw = raw.reshape(8, pairs, BF16_ROWS, 2 * count)
            at = start + group * 8
            for p in range(pairs):
                raw_c, raw_s = raw[:, p, :, :count], raw[:, p, :, count:]
                cosine, sine = cos_p[p][None], sin_p[p][None]
                real = sum_blocks(raw_c * cosine - raw_s * sine)
                imag = sum_blocks(raw_c * sine + raw_s * cosine)
                for h in range(HEMIS):
                    sums[p, h, 0, at : at + 8] = real[h]
                    sums[p, h, 1, at : at + 8] = -imag[h]

    contract(0)
    for c in range(1, len(spans)):
        copies[c].wait()
        contract(c)
        finish(c - 1)
    finish(len(spans) - 1)
    cols = HEMIS * 2 * map_count
    for j in range(count // LANES):
        lanes = slice(j * LANES, (j + 1) * LANES)
        held = [sums[p, :, :, :, lanes].reshape(cols, LANES).astype(BF16) for p in range(pairs)]
        block = dot_nt(gather, jnp.concatenate(held, axis=1))
        out_ref[j * LANES * pairs : (j + 1) * LANES * pairs] = block.astype(BF16)


def prepare_kernel(
    pairs, low_pairs, own_ref, hi_ref, lo_ref, beam_ref,
    hi_out, lo_out, weight_out, gather_out, scatter_out,
):
    slot, owned = pl.program_id(0), pl.num_programs(0)
    order = own_ref[slot]
    degrees = iota(beam_ref.shape, 1)
    sign = (1 - 2 * ((degrees + order) & 1)).astype(F32)
    weight_out[0] = jnp.where(degrees >= order, beam_ref[...], 0.0)
    for source, target in ((hi_ref, hi_out), (lo_ref, lo_out)):
        half = source.shape[1]
        target[0, :half] = source[0]
        target[0, half:] = (source[0].astype(F32) * sign).astype(BF16)

    rows, depth = gather_out.shape
    column = iota((1, depth), 1)
    hemi, pair = column // (depth // HEMIS), column % (depth // HEMIS)
    home = (pair // pairs * owned + slot) * pairs + pair % pairs + hemi * (rows // HEMIS)
    gather_out[...] = jnp.where(iota((rows, depth), 0) == home, 1.0, 0.0).astype(BF16)

    @pl.when(slot == 0)
    def _():
        shape = scatter_out.shape
        column = iota((1, shape[1]), 1)
        total = lo_ref.shape[1]
        part, pair = column // total, column % total
        home = (pair // low_pairs * owned + part) * low_pairs + pair % low_pairs
        scatter_out[...] = jnp.where(iota(shape, 0) == home, 1.0, 0.0).astype(BF16)


def inverse_table_kernel(pairs, column_ref, table_ref, gather_ref):
    count = column_ref.shape[0]
    column = column_ref[...]
    step = F32_ROWS // HEMIS * LANES
    cosine, sine = unit_circle(column * iota((count, LANES), 1) & (NPIX_LO - 1), NPIX_LO)
    cos_step, sin_step = unit_circle(
        jnp.broadcast_to(column * step & (NPIX_LO - 1), (count, LANES)), NPIX_LO
    )
    for a in range(table_ref.shape[1] // LANES):
        lanes = slice(a * LANES, (a + 1) * LANES)
        table_ref[:count, lanes] = cosine.astype(BF16)
        table_ref[count:, lanes] = (-sine).astype(BF16)
        cosine, sine = (
            cosine * cos_step - sine * sin_step,
            sine * cos_step + cosine * sin_step,
        )
    gather_ref[...] = pair_rows(pairs)


def harmonic_kernel(
    received_ref, gather_ref, scatter_ref, hi_ref, lo_ref, weight_ref, out_ref, held
):
    owned, depth = hi_ref.shape[:2]
    half = received_ref.shape[1] // HEMIS
    low_total = lo_ref.shape[1] // HEMIS
    received = jnp.concatenate([received_ref[:, :half], received_ref[:, half:]], axis=0)
    coeffs = dot_tn(received, gather_ref[...]).astype(BF16)
    for g in range(owned):
        alm = dot_nn(coeffs[:, g * depth : (g + 1) * depth], hi_ref[g]) * weight_ref[g]
        both = dot_nt(lo_ref[g], jnp.concatenate(split(alm), axis=0))
        total = (both[:, :half] + both[:, half:]).astype(BF16)
        for h in range(HEMIS):
            held[g * low_total : (g + 1) * low_total, h * half : (h + 1) * half] = total[
                h * low_total : (h + 1) * low_total
            ]
    out_ref[...] = dot_nn(scatter_ref[...], held[...]).astype(BF16)


def synthesise_kernel(
    lo_ref, orders_ref, table_ref, gather_ref, returned_ref, out_hbm,
    spectra, high, low, buf_a, buf_b, buf_c, buf_d, sems,
):
    buffers = (buf_a, buf_b, buf_c, buf_d)
    map_count, pairs, wide = buf_a.shape[:3]
    count = orders_ref.shape[1]
    orders = orders_ref[...]
    for j in range(count // LANES):
        rows = slice(j * LANES * pairs, (j + 1) * LANES * pairs)
        turned = dot_tn(returned_ref[rows], gather_ref[...])
        for p in range(pairs):
            spectra[p, :, j * LANES : (j + 1) * LANES] = turned[:, p * LANES : (p + 1) * LANES]

    scale = math.sqrt(2.0 / count)
    south = (iota((F32_ROWS, count), 0) & 1) == 1
    for p in range(pairs):
        offset = (lo_ref[p] - NSIDE_LO + 1) & 1
        step = 2 * LANES * (iota((F32_ROWS, count), 0) // HEMIS) + offset
        cosine, sine = unit_circle(orders * step & (2 * NPIX_LO - 1), 2 * NPIX_LO)
        cosine, sine = cosine * scale, sine * scale

        def turn(i):
            def spread(c):
                north = spectra[p, c * map_count + i : c * map_count + i + 1]
                at = (2 + c) * map_count + i
                return jnp.where(south, spectra[p, at : at + 1], north)

            real, imag = spread(0), spread(1)
            return real * cosine - imag * sine, imag * cosine + real * sine

        for i in range(0, map_count, 2):
            at = slice((p * map_count + i) * F32_ROWS, (p * map_count + i + 2) * F32_ROWS)
            for c, parts in enumerate(zip(turn(i), turn(i + 1))):
                lanes = slice(c * count, (c + 1) * count)
                high[at, lanes], low[at, lanes] = split(jnp.concatenate(parts, axis=0))

    copies = []
    for n, buffer in enumerate(buffers):
        table = table_ref[:, n * wide * LANES : (n + 1) * wide * LANES]
        pixels = dot_nn(high[...], table) + dot_nn(low[...], table)
        pixels = pixels.reshape(pairs, map_count, F32_ROWS, wide * LANES)
        for p in range(pairs):
            for a in range(wide):
                buffer[:, p, a] = pixels[p, :, :, a * LANES : (a + 1) * LANES]
        target = out_hbm.at[:, :, pl.ds(n * wide, wide)]
        copies.append(pltpu.make_async_copy(buffer, target, sems.at[n]))
        copies[-1].start()
    for copy in copies:
        copy.wait()


def vmem():
    return pl.BlockSpec(memory_space=pltpu.VMEM)


def smem():
    return pl.BlockSpec(memory_space=pltpu.SMEM)


def hbm():
    return pl.BlockSpec(memory_space=pltpu.HBM)


def params(mebibytes):
    return pltpu.CompilerParams(vmem_limit_bytes=mebibytes * 2**20)


def struct(shape, dtype):
    return jax.ShapeDtypeStruct(shape, dtype)


def per_device(
    sky_maps, hi_cycles, lo_cycles, azimuth_orders, legendre_hi, legendre_lo, beam_weights
):
    axes = ("band", "ma")
    map_count, pairs = sky_maps.shape[:2]
    low_pairs = lo_cycles.shape[0]
    count = azimuth_orders.shape[0]
    owned, degree_count, pair_total = legendre_hi.shape
    low_total = legendre_lo.shape[2]
    devices = count // owned
    order_row = azimuth_orders.reshape(1, count)
    order_column = azimuth_orders.reshape(count, 1)
    cols = HEMIS * 2 * map_count

    inner = BF16_ROWS // HEMIS
    blocks = NPIX_HI // (inner * LANES)
    sky = sky_maps.reshape(map_count, pairs, HEMIS, blocks, inner, LANES)
    sky = sky.transpose(0, 1, 3, 4, 2, 5)
    sky = sky.reshape(map_count * pairs, blocks, BF16_ROWS, LANES)
    quarter = map_count // 4
    spans = [(k * quarter, quarter) for k in range(3)]
    spans += [(3 * quarter, quarter // 2), (3 * quarter + quarter // 2, quarter // 2)]
    raw = pltpu.VMEM((quarter * pairs * BF16_ROWS, 2 * count), F32)
    outgoing = pl.pallas_call(
        functools.partial(analyse_kernel, spans),
        out_shape=struct((count * pairs, cols), BF16),
        in_specs=[hbm(), hbm(), hbm()],
        out_specs=vmem(),
        scratch_shapes=[
            pltpu.SMEM((pairs,), jnp.int32),
            pltpu.VMEM((1, count), jnp.int32),
            pltpu.VMEM((map_count * pairs, blocks, BF16_ROWS, LANES), BF16),
            pltpu.VMEM((blocks * LANES, 2 * count), BF16),
            raw,
            raw,
            pltpu.VMEM((pairs, HEMIS, 2, map_count, count), F32),
            pltpu.SemaphoreType.DMA((2 + len(spans),)),
        ],
        compiler_params=params(40),
        name="analyse",
    )(hi_cycles, order_row, sky)
    received = lax.all_to_all(
        outgoing.reshape(devices, owned * pairs, cols), axes, split_axis=0, concat_axis=0, tiled=True
    )

    own = lax.dynamic_slice_in_dim(azimuth_orders, lax.axis_index(axes) * owned, owned)
    rows, low_rows = count * pairs, count * low_pairs
    depth, low_depth = HEMIS * pair_total, HEMIS * low_total
    work = owned * degree_count * (depth + low_depth)
    hi_table, lo_table, weights, gather, scatter = pl.pallas_call(
        functools.partial(prepare_kernel, pairs, low_pairs),
        grid=(owned,),
        out_shape=[
            struct((owned, depth, degree_count), BF16),
            struct((owned, low_depth, degree_count), BF16),
            struct((owned, 1, degree_count), F32),
            struct((HEMIS * rows, owned * depth), BF16),
            struct((low_rows, owned * low_total), BF16),
        ],
        in_specs=[
            smem(),
            pl.BlockSpec((1, pair_total, degree_count), lambda g: (g, 0, 0)),
            pl.BlockSpec((1, low_total, degree_count), lambda g: (g, 0, 0)),
            pl.BlockSpec((1, degree_count), lambda g: (0, 0)),
        ],
        out_specs=[
            pl.BlockSpec((1, depth, degree_count), lambda g: (g, 0, 0)),
            pl.BlockSpec((1, low_depth, degree_count), lambda g: (g, 0, 0)),
            pl.BlockSpec((1, 1, degree_count), lambda g: (g, 0, 0)),
            pl.BlockSpec((HEMIS * rows, depth), lambda g: (0, g)),
            pl.BlockSpec((low_rows, owned * low_total), lambda g: (0, 0)),
        ],
        compiler_params=params(24),
        cost_estimate=pl.CostEstimate(flops=8 * work, bytes_accessed=4 * work, transcendentals=0),
        name="prepare",
    )(
        own,
        legendre_hi.transpose(0, 2, 1),
        legendre_lo.transpose(0, 2, 1),
        beam_weights.reshape(1, degree_count),
    )
    synthesised = pl.pallas_call(
        harmonic_kernel,
        out_shape=struct((low_rows, cols), BF16),
        in_specs=[vmem()] * 6,
        out_specs=vmem(),
        scratch_shapes=[pltpu.VMEM((owned * low_total, cols), BF16)],
        compiler_params=params(16),
        name="harmonic",
    )(received.reshape(rows, cols), gather, scatter, hi_table, lo_table, weights)
    returned = lax.all_to_all(
        synthesised.reshape(devices, owned * low_pairs, cols),
        axes,
        split_axis=0,
        concat_axis=0,
        tiled=True,
    )

    blocks_lo = NPIX_LO // (F32_ROWS // HEMIS * LANES)
    side = LANES * low_pairs
    inverse_table, regroup = pl.pallas_call(
        functools.partial(inverse_table_kernel, low_pairs),
        out_shape=[struct((2 * count, blocks_lo * LANES), BF16), struct((side, side), BF16)],
        in_specs=[vmem()],
        out_specs=[vmem(), vmem()],
        compiler_params=params(8),
        cost_estimate=pl.CostEstimate(
            flops=64 * count * blocks_lo * LANES,
            bytes_accessed=8 * count * blocks_lo * LANES,
            transcendentals=0,
        ),
        name="inverse_table",
    )(order_column)
    steps = 4
    wide = blocks_lo // steps
    buffer = pltpu.VMEM((map_count, low_pairs, wide, F32_ROWS, LANES), F32)
    spectrum = pltpu.VMEM((map_count * low_pairs * F32_ROWS, 2 * count), BF16)
    pixels = pl.pallas_call(
        synthesise_kernel,
        out_shape=struct((map_count, low_pairs, blocks_lo, F32_ROWS, LANES), F32),
        in_specs=[smem(), vmem(), vmem(), vmem(), vmem()],
        out_specs=hbm(),
        scratch_shapes=[
            pltpu.VMEM((low_pairs, cols, count), F32),
            spectrum,
            spectrum,
            buffer,
            buffer,
            buffer,
            buffer,
            pltpu.SemaphoreType.DMA((steps,)),
        ],
        compiler_params=params(32),
        name="synthesise",
    )(lo_cycles, order_row, inverse_table, regroup, returned.reshape(low_rows, cols))
    pixels = pixels.reshape(map_count, low_pairs, blocks_lo, F32_ROWS // HEMIS, HEMIS, LANES)
    pixels = pixels.transpose(0, 1, 4, 2, 3, 5)
    return pixels.reshape(map_count, low_pairs, HEMIS, NPIX_LO)


def solution(mesh):
    spread = ("band", "ma")
    return jax.shard_map(
        per_device,
        mesh=mesh,
        in_specs=(
            P(None, spread, None, None),
            P(spread),
            P(spread),
            P(),
            P(spread, None, None),
            P(spread, None, None),
            P(),
        ),
        out_specs=P(None, spread, None, None),
        check_vma=False,
    )
```

time: 51 us -> 50.9 us (level)
  waiting for transfers between devices: 15.4 us -> 8.08 us
  local copies, waits for them, and re-layouts: 6.91 us -> 13.1 us
  starting transfers between devices: 9.9 us -> 12.3 us
  Pallas kernels: 18.4 us -> 17 us
    unnamed x16 -> x24, local copies, waits for them, and re-layouts: 4.71 us -> 12.9 us
    all_to_all x2, waiting for transfers between devices: 15.4 us -> 8.08 us  [the longest x1 7.22 us: per_device(): lax.all_to_all(synthesised.reshape(devices, owned * low_pairs, cols), axe...]
    all_to_all x2, starting transfers between devices: 9.9 us -> 12.3 us  [the longest x1 7.33 us: per_device(): lax.all_to_all(outgoing.reshape(devices, owned * pairs, cols), axes, spli...]
    reshape x4 -> x0, local copies, waits for them, and re-layouts: 1.78 us -> none  [the longest x2 0.85 us: per_device(): synthesised.transpose(0, 2, 1, 3).reshape(owned, low_total, cols)]
    pallas_call x3 -> x5, Pallas kernels: 18.4 us -> 17 us  [the longest x1 7.07 us: per_device(): pl.pallas_call(functools.partial(analyse_kernel, spans), out_shape=struct...]
  transfers between devices with their start and end apart: 2 -> 2, of which waited for: 2 -> 2; matrix products, arithmetic and copies ran while one was open for 0% -> 0% of each run, Pallas kernels for 0% -> 4%
where the time goes in v2:
time: 50.9 us; the launch traced here: 50.5 us
  Pallas kernels  17 us (33%)
  local copies, waits for them, and re-layouts  13.1 us (26%)
  starting transfers between devices  12.3 us (24%)
  waiting for transfers between devices  8.08 us (16%)
    unnamed x24, local copies, waits for them, and re-layouts  12.9 us
    all_to_all x1, starting transfers between devices, per_device(): lax.all_to_all(outgoing.reshape(devices, owned * pairs, cols), axes, spli...  7.33 us
    all_to_all x1, waiting for transfers between devices, per_device(): lax.all_to_all(synthesised.reshape(devices, owned * low_pairs, cols), axe...  7.22 us
    pallas_call x1, Pallas kernels, per_device(): pl.pallas_call(functools.partial(analyse_kernel, spans), out_shape=struct...  7.07 us
    all_to_all x1, starting transfers between devices, per_device(): lax.all_to_all(synthesised.reshape(devices, owned * low_pairs, cols), axe...  4.99 us
    pallas_call x1, Pallas kernels, per_device(): pl.pallas_call(harmonic_kernel, out_shape=struct((low_rows, cols), BF16),...  4.14 us
    pallas_call x1, Pallas kernels, per_device(): pl.pallas_call(synthesise_kernel, out_shape=struct((map_count, low_pairs,...  3.72 us
    pallas_call x1, Pallas kernels, per_device(): pl.pallas_call(functools.partial(prepare_kernel, pairs, low_pairs), grid=...  1.57 us
  transfers between devices with their start and end apart: 2, of which 2 were waited for; matrix products, arithmetic and copies ran while one was open for 0% of the time, Pallas kernels for 4%

profile of v2, /device:TPU:0, one launch (start us, length us, event | category | flops | bytes accessed | tf_op | source)
XLA Modules:
  0.0 50.5 jit_solution(8215598776366768074)
XLA Ops:
  0.0 0.0 copy-start
  0.0 3.4 %copy-done = bf16[64,2,2,16384]{3,2,1,0:T(2,128)(2,1)S(1)} copy-done((bf16[64,2,2,16384]{3,2,1,0:T(2,128)(2,1)S(1)}, bf16[64,2,2,16384]{3,2,1,0:T(2,128)(2,1)}, u32[]{:S(2)}) %copy-start) | copy-done | bytes 8388632
  3.4 0.0 copy-start.8
  3.4 0.7 %copy-done.8 = s32[128]{0:T(128)S(1)} copy-done((s32[128]{0:T(128)S(1)}, s32[128]{0:T(128)}, u32[]{:S(2)}) %copy-start.8) | copy-done | bytes 536
  4.0 0.0 copy-start.10
  4.0 0.7 %copy-done.10 = s32[2]{0:T(128)S(1)} copy-done((s32[2]{0:T(128)S(1)}, s32[2]{0:T(128)}, u32[]{:S(2)}) %copy-start.10) | copy-done | bytes 32
  4.7 0.0 copy-start.9
  4.7 0.0 copy-start.7
  4.7 7.1 %analyse.1 = bf16[256,256]{1,0:T(8,128)(2,1)} custom-call(s32[2]{0:T(128)S(1)} %copy-done.10, s32[1,128]{1,0:T(1,128)S(1)} %bitcast.25, bf16[128,16,16,128]{3,2,1,0:T(8,128)(2,1)S(1)} %bitcast.19), custom_call_target="tpu_custom_call" | custom-call | tf_op jit(solution)/shard_map/analyse/pallas_call | solution.py:337
  11.8 7.3 %all-to-all-start = ((bf16[32,8,256]{2,1,0:T(8,128)(2,1)}), bf16[32,8,256]{2,1,0:T(8,128)(2,1)S(1)}, u32[]{:S(2)}, u32[]{:S(2)}) async-start(bf16[32,8,256]{2,1,0:T(8,128)(2,1)} %bitcast.5), calls=%async_computation | async-start | bytes 262144 | tf_op jit(solution)/shard_map/all_to_all | solution.py:355
  19.1 0.0 copy-done.9
  19.1 0.1 dynamic_slice.3.own_ref
  19.2 0.0 copy-done.7
  19.2 0.0 copy-start.3
  19.2 1.4 %copy-done.3 = bf16[4,3072,64]{1,2,0:T(8,128)(2,1)S(1)} copy-done((bf16[4,3072,64]{1,2,0:T(8,128)(2,1)S(1)}, bf16[4,3072,64]{1,2,0:T(8,128)(2,1)}, u32[]{:S(2)}) %copy-start.3) | copy-done | bytes 1572888
  20.6 0.0 copy-start.4
  20.6 1.4 %copy-done.4 = bf16[4,3072,64]{1,2,0:T(8,128)(2,1)S(1)} copy-done((bf16[4,3072,64]{1,2,0:T(8,128)(2,1)S(1)}, bf16[4,3072,64]{1,2,0:T(8,128)(2,1)}, u32[]{:S(2)}) %copy-start.4) | copy-done | bytes 1572888
  22.0 1.6 %prepare.1 = (bf16[4,128,3072]{2,1,0:T(8,128)(2,1)S(1)}, bf16[4,128,3072]{2,1,0:T(8,128)(2,1)S(1)}, f32[4,1,3072]{2,1,0:T(1,128)S(1)}, bf16[512,512]{1,0:T(8,128)(2,1)S(1)}, bf16[256,256]{1,0:T(8,128)(2,1)S(1)}) custom-call(s32[4]{0:T(128)S(1)} %dynamic_slice.3.own_ref, bf16[4,64,3072]{2,1,0:T(8,128)(2,1)S(1)} %bitcast.20, ...), custom_call_target="tpu_custom_call" | custom-call | flops 25165824 | bytes 12582912 | tf_op jit(solution)/shard_map/prepare/pallas_call | solution.py:363
  23.6 0.0 copy-start.1
  23.6 1.7 %copy-done.1 = bf16[4,128,3072]{2,1,0:T(8,128)(2,1)} copy-done((bf16[4,128,3072]{2,1,0:T(8,128)(2,1)}, bf16[4,128,3072]{2,1,0:T(8,128)(2,1)S(1)}, u32[]{:S(2)}) %copy-start.1) | copy-done | bytes 3145752
  25.3 0.0 copy-start.5
  25.3 0.8 %copy-done.5 = bf16[512,512]{1,0:T(8,128)(2,1)} copy-done((bf16[512,512]{1,0:T(8,128)(2,1)}, bf16[512,512]{1,0:T(8,128)(2,1)S(1)}, u32[]{:S(2)}) %copy-start.5) | copy-done | bytes 524312
  26.1 0.9 %all-to-all-done = bf16[32,8,256]{2,1,0:T(8,128)(2,1)S(1)} async-done(((bf16[32,8,256]{2,1,0:T(8,128)(2,1)}), bf16[32,8,256]{2,1,0:T(8,128)(2,1)S(1)}, u32[]{:S(2)}, u32[]{:S(2)}) %all-to-all-start) | async-done | bytes 131104 | tf_op jit(solution)/shard_map/all_to_all | solution.py:355
  26.9 0.0 copy-start.2
  26.9 1.9 %copy-done.2 = bf16[4,128,3072]{2,1,0:T(8,128)(2,1)S(1)} copy-done((bf16[4,128,3072]{2,1,0:T(8,128)(2,1)S(1)}, bf16[4,128,3072]{2,1,0:T(8,128)(2,1)}, u32[]{:S(2)}) %copy-start.2) | copy-done | bytes 3145752
  28.8 0.0 copy-start.6
  28.8 1.0 %copy-done.6 = bf16[512,512]{1,0:T(8,128)(2,1)S(1)} copy-done((bf16[512,512]{1,0:T(8,128)(2,1)S(1)}, bf16[512,512]{1,0:T(8,128)(2,1)}, u32[]{:S(2)}) %copy-start.6) | copy-done | bytes 524312
  29.9 0.0 copy-start.11
  29.9 4.1 %harmonic.1 = bf16[256,256]{1,0:T(8,128)(2,1)} custom-call(bf16[256,256]{1,0:T(8,128)(2,1)S(1)} %bitcast.22, bf16[512,512]{1,0:T(8,128)(2,1)S(1)} %copy-done.6, bf16[256,256]{1,0:T(8,128)(2,1)S(1)} %get-tuple-element.15.scatter_ref, bf16[4,128,3072]{2,1,0:T(8,128)(2,1)S(1)} %get-tuple-element.16.hi_ref, bf16[4,128,3072]{2,1,0:T(8,128)(2,1)S(1)} %copy-done.2, ...), custom_call_target="tpu_custom_call" | custom-call | tf_op jit(solution)/shard_map/harmonic/pallas_call | solution.py:395
  34.0 5.0 %all-to-all-start.1 = ((bf16[32,8,256]{2,1,0:T(8,128)(2,1)}), bf16[32,8,256]{2,1,0:T(8,128)(2,1)S(1)}, u32[]{:S(2)}, u32[]{:S(2)}) async-start(bf16[32,8,256]{2,1,0:T(8,128)(2,1)} %bitcast.10), calls=%async_computation.1 | async-start | bytes 262144 | tf_op jit(solution)/shard_map/all_to_all | solution.py:404
  39.0 0.1 copy.8.column_ref
  39.1 0.5 inverse_table.1
  39.6 7.2 %all-to-all-done.1 = bf16[32,8,256]{2,1,0:T(8,128)(2,1)S(1)} async-done(((bf16[32,8,256]{2,1,0:T(8,128)(2,1)}), bf16[32,8,256]{2,1,0:T(8,128)(2,1)S(1)}, u32[]{:S(2)}, u32[]{:S(2)}) %all-to-all-start.1) | async-done | bytes 131104 | tf_op jit(solution)/shard_map/all_to_all | solution.py:404
  46.8 0.0 copy-done.11
  46.8 3.7 %synthesise.1 = f32[64,2,8,8,128]{4,3,2,1,0:T(8,128)} custom-call(s32[2]{0:T(128)S(1)} %copy-done.11, s32[1,128]{1,0:T(1,128)S(1)} %bitcast.27, bf16[256,1024]{1,0:T(8,128)(2,1)S(1)} %get-tuple-element.12.table_ref, bf16[256,256]{1,0:T(8,128)(2,1)S(1)} %get-tuple-element.13.gather_ref, bf16[256,256]{1,0:T(8,128)(2,1)S(1)} %bitcast.23), custom_call_target="tpu_custom_call" | custom-call | tf_op jit(solution)/shard_map/synthesise/pallas_call | solution.py:431
Async XLA Ops:
  0.0 3.4 %copy-start = (bf16[64,2,2,16384]{3,2,1,0:T(2,128)(2,1)S(1)}, bf16[64,2,2,16384]{3,2,1,0:T(2,128)(2,1)}, u32[]{:S(2)}) copy-start(bf16[64,2,2,16384]{3,2,1,0:T(2,128)(2,1)} %param.7) | copy-start | bytes 25165828
  3.4 0.7 %copy-start.8 = (s32[128]{0:T(128)S(1)}, s32[128]{0:T(128)}, u32[]{:S(2)}) copy-start(s32[128]{0:T(128)} %param.10) | copy-start | bytes 1540
  4.0 0.7 %copy-start.10 = (s32[2]{0:T(128)S(1)}, s32[2]{0:T(128)}, u32[]{:S(2)}) copy-start(s32[2]{0:T(128)} %hi_hbm.1) | copy-start | bytes 28
  4.7 14.4 %copy-start.9 = (s32[128]{0:T(128)S(1)}, s32[128]{0:T(128)}, u32[]{:S(2)}) copy-start(s32[128]{0:T(128)} %param.10) | copy-start | bytes 1540
  4.7 14.5 %copy-start.7 = (f32[3072]{0:T(1024)S(1)}, f32[3072]{0:T(1024)}, u32[]{:S(2)}) copy-start(f32[3072]{0:T(1024)} %param.13) | copy-start | bytes 36868
  11.8 15.1 %all-to-all-start = ((bf16[32,8,256]{2,1,0:T(8,128)(2,1)}), bf16[32,8,256]{2,1,0:T(8,128)(2,1)S(1)}, u32[]{:S(2)}, u32[]{:S(2)}) async-start(bf16[32,8,256]{2,1,0:T(8,128)(2,1)} %bitcast.5), calls=%async_computation | async-start | bytes 262144 | tf_op jit(solution)/shard_map/all_to_all | solution.py:355
  19.2 1.4 %copy-start.3 = (bf16[4,3072,64]{1,2,0:T(8,128)(2,1)S(1)}, bf16[4,3072,64]{1,2,0:T(8,128)(2,1)}, u32[]{:S(2)}) copy-start(bf16[4,3072,64]{1,2,0:T(8,128)(2,1)} %param.11) | copy-start | bytes 4718596
  20.6 1.4 %copy-start.4 = (bf16[4,3072,64]{1,2,0:T(8,128)(2,1)S(1)}, bf16[4,3072,64]{1,2,0:T(8,128)(2,1)}, u32[]{:S(2)}) copy-start(bf16[4,3072,64]{1,2,0:T(8,128)(2,1)} %param.12) | copy-start | bytes 4718596
  23.6 1.7 %copy-start.1 = (bf16[4,128,3072]{2,1,0:T(8,128)(2,1)}, bf16[4,128,3072]{2,1,0:T(8,128)(2,1)S(1)}, u32[]{:S(2)}) copy-start(bf16[4,128,3072]{2,1,0:T(8,128)(2,1)S(1)} %get-tuple-element.17.lo_ref) | copy-start | bytes 9437188
  25.3 0.8 %copy-start.5 = (bf16[512,512]{1,0:T(8,128)(2,1)}, bf16[512,512]{1,0:T(8,128)(2,1)S(1)}, u32[]{:S(2)}) copy-start(bf16[512,512]{1,0:T(8,128)(2,1)S(1)} %get-tuple-element.14.gather_ref) | copy-start | bytes 1572868
  26.9 1.9 %copy-start.2 = (bf16[4,128,3072]{2,1,0:T(8,128)(2,1)S(1)}, bf16[4,128,3072]{2,1,0:T(8,128)(2,1)}, u32[]{:S(2)}) copy-start(bf16[4,128,3072]{2,1,0:T(8,128)(2,1)} %copy-done.1) | copy-start | bytes 9437188
  28.8 1.0 %copy-start.6 = (bf16[512,512]{1,0:T(8,128)(2,1)S(1)}, bf16[512,512]{1,0:T(8,128)(2,1)}, u32[]{:S(2)}) copy-start(bf16[512,512]{1,0:T(8,128)(2,1)} %copy-done.5) | copy-start | bytes 1572868
  29.9 17.0 %copy-start.11 = (s32[2]{0:T(128)S(1)}, s32[2]{0:T(128)}, u32[]{:S(2)}) copy-start(s32[2]{0:T(128)} %lo_ref.1) | copy-start | bytes 28
  34.0 12.8 %all-to-all-start.1 = ((bf16[32,8,256]{2,1,0:T(8,128)(2,1)}), bf16[32,8,256]{2,1,0:T(8,128)(2,1)S(1)}, u32[]{:S(2)}, u32[]{:S(2)}) async-start(bf16[32,8,256]{2,1,0:T(8,128)(2,1)} %bitcast.10), calls=%async_computation.1 | async-start | bytes 262144 | tf_op jit(solution)/shard_map/all_to_all | solution.py:404

commit v3 on v2

--- a/solution.py
+++ b/solution.py
@@ -16,6 +16,7 @@
 LANES = 128
 HEMIS = 2
 BF16_ROWS = 16
+WHOLE_VMEM = 67_043_328
 F32_ROWS = 8
 F32 = jnp.float32
 BF16 = jnp.bfloat16
@@ -123,7 +124,9 @@
         rows = jnp.concatenate(
             [sky[part, a].reshape(size * pairs * BF16_ROWS, LANES) for a in range(blocks)], axis=1
         )
-        raws[c % 2][: size * pairs * BF16_ROWS] = dot_nn(rows, table[...])
+        half = blocks * LANES // 2
+        raw = dot_nn(rows[:, :half], table[:half]) + dot_nn(rows[:, half:], table[half:])
+        raws[c % 2][: size * pairs * BF16_ROWS] = raw
 
     sub = iota((1, F32_ROWS, count), 1)
 
@@ -171,38 +174,18 @@
         out_ref[j * LANES * pairs : (j + 1) * LANES * pairs] = block.astype(BF16)
 
 
-def prepare_kernel(
-    pairs, low_pairs, own_ref, hi_ref, lo_ref, beam_ref,
-    hi_out, lo_out, weight_out, gather_out, scatter_out,
+def inverse_table_kernel(
+    pairs, lo_ref, orders_ref, column_ref, table_ref, gather_ref, phase_ref
 ):
-    slot, owned = pl.program_id(0), pl.num_programs(0)
-    order = own_ref[slot]
-    degrees = iota(beam_ref.shape, 1)
-    sign = (1 - 2 * ((degrees + order) & 1)).astype(F32)
-    weight_out[0] = jnp.where(degrees >= order, beam_ref[...], 0.0)
-    for source, target in ((hi_ref, hi_out), (lo_ref, lo_out)):
-        half = source.shape[1]
-        target[0, :half] = source[0]
-        target[0, half:] = (source[0].astype(F32) * sign).astype(BF16)
-
-    rows, depth = gather_out.shape
-    column = iota((1, depth), 1)
-    hemi, pair = column // (depth // HEMIS), column % (depth // HEMIS)
-    home = (pair // pairs * owned + slot) * pairs + pair % pairs + hemi * (rows // HEMIS)
-    gather_out[...] = jnp.where(iota((rows, depth), 0) == home, 1.0, 0.0).astype(BF16)
-
-    @pl.when(slot == 0)
-    def _():
-        shape = scatter_out.shape
-        column = iota((1, shape[1]), 1)
-        total = lo_ref.shape[1]
-        part, pair = column // total, column % total
-        home = (pair // low_pairs * owned + part) * low_pairs + pair % low_pairs
-        scatter_out[...] = jnp.where(iota(shape, 0) == home, 1.0, 0.0).astype(BF16)
-
-
-def inverse_table_kernel(pairs, column_ref, table_ref, gather_ref):
     count = column_ref.shape[0]
+    orders = orders_ref[...]
+    scale = math.sqrt(2.0 / count)
+    for p in range(pairs):
+        offset = (lo_ref[p] - NSIDE_LO + 1) & 1
+        step = 2 * LANES * (iota((F32_ROWS, count), 0) // HEMIS) + offset
+        cosine, sine = unit_circle(orders * step & (2 * NPIX_LO - 1), 2 * NPIX_LO)
+        phase_ref[p, 0] = cosine * scale
+        phase_ref[p, 1] = sine * scale
     column = column_ref[...]
     step = F32_ROWS // HEMIS * LANES
     cosine, sine = unit_circle(column * iota((count, LANES), 1) & (NPIX_LO - 1), NPIX_LO)
@@ -220,46 +203,77 @@
     gather_ref[...] = pair_rows(pairs)
 
 
+def slot_rows(owned, pairs, pair_total):
+    shape = (pair_total * owned, owned * pair_total)
+    column = iota((1, shape[1]), 1)
+    slot, pair = column // pair_total, column % pair_total
+    home = (pair // pairs * owned + slot) * pairs + pair % pairs
+    return jnp.where(iota(shape, 0) == home, 1.0, 0.0).astype(BF16)
+
+
+def prepare_kernel(pairs, own_ref, beam_ref, weight_ref, sign_ref, gather_ref):
+    degrees = iota(beam_ref.shape, 1)
+    for g in range(weight_ref.shape[0]):
+        order = own_ref[g]
+        weight_ref[g] = jnp.where(degrees >= order, beam_ref[...], 0.0)
+        sign_ref[g] = (1 - 2 * ((degrees + order) & 1)).astype(F32).astype(BF16)
+    owned = weight_ref.shape[0]
+    gather_ref[...] = slot_rows(owned, pairs, gather_ref.shape[0] // owned)
+
+
 def harmonic_kernel(
-    received_ref, gather_ref, scatter_ref, hi_ref, lo_ref, weight_ref, out_ref, held
+    same, pairs, low_pairs, received_ref, weight_ref, sign_ref, gather_ref, hi_hbm, lo_hbm,
+    out_ref, hi_ref, lo_ref, held, sems,
 ):
-    owned, depth = hi_ref.shape[:2]
+    owned, pair_total = hi_ref.shape[:2]
+    low_total = lo_ref.shape[1]
     half = received_ref.shape[1] // HEMIS
-    low_total = lo_ref.shape[1] // HEMIS
-    received = jnp.concatenate([received_ref[:, :half], received_ref[:, half:]], axis=0)
-    coeffs = dot_tn(received, gather_ref[...]).astype(BF16)
+    copies = []
     for g in range(owned):
-        alm = dot_nn(coeffs[:, g * depth : (g + 1) * depth], hi_ref[g]) * weight_ref[g]
-        both = dot_nt(lo_ref[g], jnp.concatenate(split(alm), axis=0))
+        copies.append(
+            [
+                pltpu.make_async_copy(source.at[g], target.at[g], sems.at[k, g])
+                for k, (source, target) in enumerate(((hi_hbm, hi_ref), (lo_hbm, lo_ref)))
+            ]
+        )
+        for copy in copies[g]:
+            copy.start()
+    north = dot_tn(received_ref[:, :half], gather_ref[...])
+    south = dot_tn(received_ref[:, half:], gather_ref[...])
+    for g in range(owned):
+        lanes = slice(g * pair_total, (g + 1) * pair_total)
+        coeffs = jnp.concatenate([north[:, lanes], south[:, lanes]], axis=1).astype(BF16)
+        for copy in copies[g]:
+            copy.wait()
+        hi_table = jnp.concatenate([hi_ref[g], hi_ref[g] * sign_ref[g]], axis=0)
+        alm = dot_nn(coeffs, hi_table) * weight_ref[g]
+        lo_table = jnp.concatenate([lo_ref[g], lo_ref[g] * sign_ref[g]], axis=0)
+        both = dot_nt(lo_table, jnp.concatenate(split(alm), axis=0))
         total = (both[:, :half] + both[:, half:]).astype(BF16)
         for h in range(HEMIS):
             held[g * low_total : (g + 1) * low_total, h * half : (h + 1) * half] = total[
                 h * low_total : (h + 1) * low_total
             ]
-    out_ref[...] = dot_nn(scatter_ref[...], held[...]).astype(BF16)
+    scatter = gather_ref[...] if same else slot_rows(owned, low_pairs, low_total)
+    out_ref[...] = dot_nn(scatter, held[...]).astype(BF16)
 
 
 def synthesise_kernel(
-    lo_ref, orders_ref, table_ref, gather_ref, returned_ref, out_hbm,
+    phase_ref, table_ref, gather_ref, returned_ref, out_hbm,
     spectra, high, low, buf_a, buf_b, buf_c, buf_d, sems,
 ):
     buffers = (buf_a, buf_b, buf_c, buf_d)
     map_count, pairs, wide = buf_a.shape[:3]
-    count = orders_ref.shape[1]
-    orders = orders_ref[...]
+    count = phase_ref.shape[3]
     for j in range(count // LANES):
         rows = slice(j * LANES * pairs, (j + 1) * LANES * pairs)
         turned = dot_tn(returned_ref[rows], gather_ref[...])
         for p in range(pairs):
             spectra[p, :, j * LANES : (j + 1) * LANES] = turned[:, p * LANES : (p + 1) * LANES]
 
-    scale = math.sqrt(2.0 / count)
     south = (iota((F32_ROWS, count), 0) & 1) == 1
     for p in range(pairs):
-        offset = (lo_ref[p] - NSIDE_LO + 1) & 1
-        step = 2 * LANES * (iota((F32_ROWS, count), 0) // HEMIS) + offset
-        cosine, sine = unit_circle(orders * step & (2 * NPIX_LO - 1), 2 * NPIX_LO)
-        cosine, sine = cosine * scale, sine * scale
+        cosine, sine = phase_ref[p, 0], phase_ref[p, 1]
 
         def turn(i):
             def spread(c):
@@ -303,8 +317,8 @@
     return pl.BlockSpec(memory_space=pltpu.HBM)
 
 
-def params(mebibytes):
-    return pltpu.CompilerParams(vmem_limit_bytes=mebibytes * 2**20)
+def params(grant=WHOLE_VMEM):
+    return pltpu.CompilerParams(vmem_limit_bytes=grant)
 
 
 def struct(shape, dtype):
@@ -349,58 +363,53 @@
             pltpu.VMEM((pairs, HEMIS, 2, map_count, count), F32),
             pltpu.SemaphoreType.DMA((2 + len(spans),)),
         ],
-        compiler_params=params(40),
+        compiler_params=params(),
         name="analyse",
     )(hi_cycles, order_row, sky)
     received = lax.all_to_all(
         outgoing.reshape(devices, owned * pairs, cols), axes, split_axis=0, concat_axis=0, tiled=True
     )
 
+    rows = count * pairs
     own = lax.dynamic_slice_in_dim(azimuth_orders, lax.axis_index(axes) * owned, owned)
-    rows, low_rows = count * pairs, count * low_pairs
-    depth, low_depth = HEMIS * pair_total, HEMIS * low_total
-    work = owned * degree_count * (depth + low_depth)
-    hi_table, lo_table, weights, gather, scatter = pl.pallas_call(
-        functools.partial(prepare_kernel, pairs, low_pairs),
-        grid=(owned,),
+    low_rows = count * low_pairs
+    same = (low_pairs, low_total) == (pairs, pair_total)
+    weights, signs, gather = pl.pallas_call(
+        functools.partial(prepare_kernel, pairs),
         out_shape=[
-            struct((owned, depth, degree_count), BF16),
-            struct((owned, low_depth, degree_count), BF16),
             struct((owned, 1, degree_count), F32),
-            struct((HEMIS * rows, owned * depth), BF16),
-            struct((low_rows, owned * low_total), BF16),
+            struct((owned, 1, degree_count), BF16),
+            struct((rows, owned * pair_total), BF16),
         ],
-        in_specs=[
-            smem(),
-            pl.BlockSpec((1, pair_total, degree_count), lambda g: (g, 0, 0)),
-            pl.BlockSpec((1, low_total, degree_count), lambda g: (g, 0, 0)),
-            pl.BlockSpec((1, degree_count), lambda g: (0, 0)),
+        in_specs=[smem(), vmem()],
+        out_specs=[vmem()] * 3,
+        compiler_params=params(16 * 2**20),
+        cost_estimate=pl.CostEstimate(
+            flops=2**10 * degree_count, bytes_accessed=2**10 * degree_count, transcendentals=0
+        ),
+        name="prepare",
+    )(own, beam_weights.reshape(1, degree_count))
+    synthesised = pl.pallas_call(
+        functools.partial(harmonic_kernel, same, pairs, low_pairs),
+        out_shape=struct((low_rows, cols), BF16),
+        in_specs=[vmem(), vmem(), vmem(), vmem(), hbm(), hbm()],
+        out_specs=vmem(),
+        scratch_shapes=[
+            pltpu.VMEM((owned, pair_total, degree_count), BF16),
+            pltpu.VMEM((owned, low_total, degree_count), BF16),
+            pltpu.VMEM((owned * low_total, cols), BF16),
+            pltpu.SemaphoreType.DMA((2, owned)),
         ],
-        out_specs=[
-            pl.BlockSpec((1, depth, degree_count), lambda g: (g, 0, 0)),
-            pl.BlockSpec((1, low_depth, degree_count), lambda g: (g, 0, 0)),
-            pl.BlockSpec((1, 1, degree_count), lambda g: (g, 0, 0)),
-            pl.BlockSpec((HEMIS * rows, depth), lambda g: (0, g)),
-            pl.BlockSpec((low_rows, owned * low_total), lambda g: (0, 0)),
-        ],
-        compiler_params=params(24),
-        cost_estimate=pl.CostEstimate(flops=8 * work, bytes_accessed=4 * work, transcendentals=0),
-        name="prepare",
+        compiler_params=params(52 * 2**20),
+        name="harmonic",
     )(
-        own,
+        received.reshape(rows, cols),
+        weights,
+        signs,
+        gather,
         legendre_hi.transpose(0, 2, 1),
         legendre_lo.transpose(0, 2, 1),
-        beam_weights.reshape(1, degree_count),
-    )
-    synthesised = pl.pallas_call(
-        harmonic_kernel,
-        out_shape=struct((low_rows, cols), BF16),
-        in_specs=[vmem()] * 6,
-        out_specs=vmem(),
-        scratch_shapes=[pltpu.VMEM((owned * low_total, cols), BF16)],
-        compiler_params=params(16),
-        name="harmonic",
-    )(received.reshape(rows, cols), gather, scatter, hi_table, lo_table, weights)
+    )
     returned = lax.all_to_all(
         synthesised.reshape(devices, owned * low_pairs, cols),
         axes,
@@ -411,19 +420,23 @@
 
     blocks_lo = NPIX_LO // (F32_ROWS // HEMIS * LANES)
     side = LANES * low_pairs
-    inverse_table, regroup = pl.pallas_call(
+    inverse_table, regroup, phase = pl.pallas_call(
         functools.partial(inverse_table_kernel, low_pairs),
-        out_shape=[struct((2 * count, blocks_lo * LANES), BF16), struct((side, side), BF16)],
-        in_specs=[vmem()],
-        out_specs=[vmem(), vmem()],
-        compiler_params=params(8),
+        out_shape=[
+            struct((2 * count, blocks_lo * LANES), BF16),
+            struct((side, side), BF16),
+            struct((low_pairs, 2, F32_ROWS, count), F32),
+        ],
+        in_specs=[smem(), vmem(), vmem()],
+        out_specs=[vmem()] * 3,
+        compiler_params=params(8 * 2**20),
         cost_estimate=pl.CostEstimate(
             flops=64 * count * blocks_lo * LANES,
             bytes_accessed=8 * count * blocks_lo * LANES,
             transcendentals=0,
         ),
         name="inverse_table",
-    )(order_column)
+    )(lo_cycles, order_row, order_column)
     steps = 4
     wide = blocks_lo // steps
     buffer = pltpu.VMEM((map_count, low_pairs, wide, F32_ROWS, LANES), F32)
@@ -431,7 +444,7 @@
     pixels = pl.pallas_call(
         synthesise_kernel,
         out_shape=struct((map_count, low_pairs, blocks_lo, F32_ROWS, LANES), F32),
-        in_specs=[smem(), vmem(), vmem(), vmem(), vmem()],
+        in_specs=[vmem(), vmem(), vmem(), vmem()],
         out_specs=hbm(),
         scratch_shapes=[
             pltpu.VMEM((low_pairs, cols, count), F32),
@@ -443,9 +456,9 @@
             buffer,
             pltpu.SemaphoreType.DMA((steps,)),
         ],
-        compiler_params=params(32),
+        compiler_params=params(32 * 2**20),
         name="synthesise",
-    )(lo_cycles, order_row, inverse_table, regroup, returned.reshape(low_rows, cols))
+    )(phase, inverse_table, regroup, returned.reshape(low_rows, cols))
     pixels = pixels.reshape(map_count, low_pairs, blocks_lo, F32_ROWS // HEMIS, HEMIS, LANES)
     pixels = pixels.transpose(0, 1, 4, 2, 3, 5)
     return pixels.reshape(map_count, low_pairs, HEMIS, NPIX_LO)

time: 50.9 us -> 44.2 us (0.87)
  local copies, waits for them, and re-layouts: 13.1 us -> 1.56 us
  waiting for transfers between devices: 8.08 us -> 12.3 us
  Pallas kernels: 17 us -> 20.1 us
  starting transfers between devices: 12.3 us -> 9.92 us
    unnamed x24 -> x6, local copies, waits for them, and re-layouts: 12.9 us -> 0.72 us
    all_to_all x1, waiting for transfers between devices: 0.86 us -> 5.63 us  [per_device(): lax.all_to_all(outgoing.reshape(devices, owned * pairs, cols), axes, spli...]
    all_to_all x1, starting transfers between devices: 4.99 us -> 2.59 us  [per_device(): lax.all_to_all(synthesised.reshape(devices, owned * low_pairs, cols), axe...]
    pallas_call x2, Pallas kernels: 5.71 us -> 8.03 us  [the longest x1 7.31 us: per_device(): pl.pallas_call(functools.partial(harmonic_kernel, same, pairs, low_pairs)...]
    pallas_call x1, Pallas kernels: 7.07 us -> 7.88 us  [per_device(): pl.pallas_call(functools.partial(analyse_kernel, spans), out_shape=struct...]
    dynamic_slice x1, local copies, waits for them, and re-layouts: 0.08 us -> 0.73 us  [per_device(): lax.dynamic_slice_in_dim(azimuth_orders, lax.axis_index(axes) * owned, ow...]
    pallas_call x1, Pallas kernels: 3.72 us -> 3.13 us  [per_device(): pl.pallas_call(synthesise_kernel, out_shape=struct((map_count, low_pairs,...]
    all_to_all x1, waiting for transfers between devices: 7.22 us -> 6.66 us  [per_device(): lax.all_to_all(synthesised.reshape(devices, owned * low_pairs, cols), axe...]
  transfers between devices with their start and end apart: 2 -> 2, of which waited for: 2 -> 2; matrix products, arithmetic and copies ran while one was open for 0% -> 2% of each run, Pallas kernels for 4% -> 4%
where the time goes in v3:
time: 44.2 us; the launch traced here: 43.9 us
  Pallas kernels  20.1 us (45%)
  waiting for transfers between devices  12.3 us (28%)
  starting transfers between devices  9.92 us (22%)
  local copies, waits for them, and re-layouts  1.56 us (4%)
    pallas_call x1, Pallas kernels, per_device(): pl.pallas_call(functools.partial(analyse_kernel, spans), out_shape=struct...  7.88 us
    all_to_all x1, starting transfers between devices, per_device(): lax.all_to_all(outgoing.reshape(devices, owned * pairs, cols), axes, spli...  7.33 us
    pallas_call x1, Pallas kernels, per_device(): pl.pallas_call(functools.partial(harmonic_kernel, same, pairs, low_pairs)...  7.31 us
    all_to_all x1, waiting for transfers between devices, per_device(): lax.all_to_all(synthesised.reshape(devices, owned * low_pairs, cols), axe...  6.66 us
    all_to_all x1, waiting for transfers between devices, per_device(): lax.all_to_all(outgoing.reshape(devices, owned * pairs, cols), axes, spli...  5.63 us
    pallas_call x1, Pallas kernels, per_device(): pl.pallas_call(synthesise_kernel, out_shape=struct((map_count, low_pairs,...  3.13 us
    all_to_all x1, starting transfers between devices, per_device(): lax.all_to_all(synthesised.reshape(devices, owned * low_pairs, cols), axe...  2.59 us
    pallas_call x1, Pallas kernels, per_device(): pl.pallas_call(functools.partial(inverse_table_kernel, low_pairs), out_sh...  1.02 us
  transfers between devices with their start and end apart: 2, of which 2 were waited for; matrix products, arithmetic and copies ran while one was open for 2% of the time, Pallas kernels for 4%

profile of v3, /device:TPU:0, one launch (start us, length us, event | category | flops | bytes accessed | tf_op | source)
XLA Modules:
  0.0 43.9 jit_solution(2397893312229383308)
XLA Ops:
  0.0 7.9 %analyse.1 = bf16[256,256]{1,0:T(8,128)(2,1)} custom-call(s32[2]{0:T(128)} %hi_hbm.1, s32[1,128]{1,0:T(1,128)} %bitcast.22, bf16[128,16,16,128]{3,2,1,0:T(8,128)(2,1)} %bitcast.25), custom_call_target="tpu_custom_call" | custom-call | tf_op jit(solution)/shard_map/analyse/pallas_call | solution.py:351
  7.9 0.0 copy-start.1
  7.9 0.0 copy-start.2
  7.9 7.3 %all-to-all-start = ((bf16[32,8,256]{2,1,0:T(8,128)(2,1)}), bf16[32,8,256]{2,1,0:T(8,128)(2,1)S(1)}, u32[]{:S(2)}, u32[]{:S(2)}) async-start(bf16[32,8,256]{2,1,0:T(8,128)(2,1)} %bitcast.28), calls=%async_computation | async-start | bytes 262144 | tf_op jit(solution)/shard_map/all_to_all | solution.py:369
  15.3 0.7 %dynamic_slice.3.own_ref = s32[4]{0:T(128)S(1)} dynamic-slice(s32[128]{0:T(128)} %param.10, s32[]{:T(128)S(6)} %select_n.3), dynamic_slice_sizes={4} | dynamic-slice | bytes 36 | tf_op jit(solution)/shard_map/dynamic_slice | solution.py:374
  16.0 0.0 copy-start
  16.0 0.7 %copy-done = f32[3072]{0:T(1024)S(1)} copy-done((f32[3072]{0:T(1024)S(1)}, f32[3072]{0:T(1024)}, u32[]{:S(2)}) %copy-start) | copy-done | bytes 12312
  16.7 0.7 %prepare.1 = (f32[4,1,3072]{2,1,0:T(1,128)S(1)}, bf16[4,1,3072]{2,1,0:T(2,128)(2,1)S(1)}, bf16[256,256]{1,0:T(8,128)(2,1)S(1)}) custom-call(s32[4]{0:T(128)S(1)} %dynamic_slice.3.own_ref, f32[1,3072]{1,0:T(1,128)S(1)} %bitcast.21), custom_call_target="tpu_custom_call" | custom-call | flops 3145728 | bytes 3145728 | tf_op jit(solution)/shard_map/prepare/pallas_call | solution.py:377
  17.4 5.6 %all-to-all-done = bf16[32,8,256]{2,1,0:T(8,128)(2,1)S(1)} async-done(((bf16[32,8,256]{2,1,0:T(8,128)(2,1)}), bf16[32,8,256]{2,1,0:T(8,128)(2,1)S(1)}, u32[]{:S(2)}, u32[]{:S(2)}) %all-to-all-start) | async-done | bytes 131104 | tf_op jit(solution)/shard_map/all_to_all | solution.py:369
  23.1 7.3 %harmonic.1 = bf16[256,256]{1,0:T(8,128)(2,1)} custom-call(bf16[256,256]{1,0:T(8,128)(2,1)S(1)} %bitcast.19, f32[4,1,3072]{2,1,0:T(1,128)S(1)} %get-tuple-element.14.weight_ref, bf16[4,1,3072]{2,1,0:T(2,128)(2,1)S(1)} %get-tuple-element.15.sign_ref, bf16[256,256]{1,0:T(8,128)(2,1)S(1)} %get-tuple-element.16.gather_ref, bf16[4,64,3072]{2,1,0:T(8,128)(2,1)} %bitcast.26, ...), custom_call_target="tpu_custom_call" | custom-call | tf_op jit(solution)/shard_map/harmonic/pallas_call | solution.py:392
  30.4 2.6 %all-to-all-start.1 = ((bf16[32,8,256]{2,1,0:T(8,128)(2,1)}), bf16[32,8,256]{2,1,0:T(8,128)(2,1)S(1)}, u32[]{:S(2)}, u32[]{:S(2)}) async-start(bf16[32,8,256]{2,1,0:T(8,128)(2,1)} %bitcast.10), calls=%async_computation.1 | async-start | bytes 262144 | tf_op jit(solution)/shard_map/all_to_all | solution.py:413
  33.0 0.0 copy-done.1
  33.0 0.1 copy.8.column_ref
  33.1 0.0 copy-done.2
  33.1 1.0 %inverse_table.1 = (bf16[256,1024]{1,0:T(8,128)(2,1)S(1)}, bf16[256,256]{1,0:T(8,128)(2,1)S(1)}, f32[2,2,8,128]{3,2,1,0:T(8,128)S(1)}) custom-call(s32[2]{0:T(128)S(1)} %copy-done.2, s32[1,128]{1,0:T(1,128)S(1)} %bitcast.24, s32[128,1]{1,0:T(8,128)S(1)} %copy.8.column_ref), custom_call_target="tpu_custom_call" | custom-call | flops 8388608 | bytes 1048576 | tf_op jit(solution)/shard_map/inverse_table/pallas_call | solution.py:423
  34.1 6.7 %all-to-all-done.1 = bf16[32,8,256]{2,1,0:T(8,128)(2,1)S(1)} async-done(((bf16[32,8,256]{2,1,0:T(8,128)(2,1)}), bf16[32,8,256]{2,1,0:T(8,128)(2,1)S(1)}, u32[]{:S(2)}, u32[]{:S(2)}) %all-to-all-start.1) | async-done | bytes 131104 | tf_op jit(solution)/shard_map/all_to_all | solution.py:413
  40.8 3.1 %synthesise.1 = f32[64,2,8,8,128]{4,3,2,1,0:T(8,128)} custom-call(f32[2,2,8,128]{3,2,1,0:T(8,128)S(1)} %get-tuple-element.11.phase_ref, bf16[256,1024]{1,0:T(8,128)(2,1)S(1)} %get-tuple-element.12.table_ref, bf16[256,256]{1,0:T(8,128)(2,1)S(1)} %get-tuple-element.13.gather_ref, bf16[256,256]{1,0:T(8,128)(2,1)S(1)} %bitcast.20), custom_call_target="tpu_custom_call" | custom-call | tf_op jit(solution)/shard_map/synthesise/pallas_call | solution.py:444
Async XLA Ops:
  7.9 25.1 %copy-start.1 = (s32[128]{0:T(128)S(1)}, s32[128]{0:T(128)}, u32[]{:S(2)}) copy-start(s32[128]{0:T(128)} %param.10) | copy-start | bytes 1540
  7.9 25.2 %copy-start.2 = (s32[2]{0:T(128)S(1)}, s32[2]{0:T(128)}, u32[]{:S(2)}) copy-start(s32[2]{0:T(128)} %lo_ref.1) | copy-start | bytes 28
  7.9 15.1 %all-to-all-start = ((bf16[32,8,256]{2,1,0:T(8,128)(2,1)}), bf16[32,8,256]{2,1,0:T(8,128)(2,1)S(1)}, u32[]{:S(2)}, u32[]{:S(2)}) async-start(bf16[32,8,256]{2,1,0:T(8,128)(2,1)} %bitcast.28), calls=%async_computation | async-start | bytes 262144 | tf_op jit(solution)/shard_map/all_to_all | solution.py:369
  16.0 0.7 %copy-start = (f32[3072]{0:T(1024)S(1)}, f32[3072]{0:T(1024)}, u32[]{:S(2)}) copy-start(f32[3072]{0:T(1024)} %param.13) | copy-start | bytes 36868
  30.4 10.4 %all-to-all-start.1 = ((bf16[32,8,256]{2,1,0:T(8,128)(2,1)}), bf16[32,8,256]{2,1,0:T(8,128)(2,1)S(1)}, u32[]{:S(2)}, u32[]{:S(2)}) async-start(bf16[32,8,256]{2,1,0:T(8,128)(2,1)} %bitcast.10), calls=%async_computation.1 | async-start | bytes 262144 | tf_op jit(solution)/shard_map/all_to_all | solution.py:413

commit v4 on v3

--- a/solution.py
+++ b/solution.py
@@ -124,9 +124,9 @@
         rows = jnp.concatenate(
             [sky[part, a].reshape(size * pairs * BF16_ROWS, LANES) for a in range(blocks)], axis=1
         )
-        half = blocks * LANES // 2
-        raw = dot_nn(rows[:, :half], table[:half]) + dot_nn(rows[:, half:], table[half:])
-        raws[c % 2][: size * pairs * BF16_ROWS] = raw
+        full = size * pairs * BF16_ROWS
+        raws[c % 2][: full // 2] = dot_nn(rows[: full // 2], table[...])
+        raws[c % 2][full // 2 : full] = dot_nn(rows[full // 2 :], table[...])
 
     sub = iota((1, F32_ROWS, count), 1)
 
@@ -211,45 +211,42 @@
     return jnp.where(iota(shape, 0) == home, 1.0, 0.0).astype(BF16)
 
 
-def prepare_kernel(pairs, own_ref, beam_ref, weight_ref, sign_ref, gather_ref):
+def prepare_kernel(
+    pairs, own_ref, beam_ref, hi_hbm, lo_hbm, weight_ref, sign_ref, gather_ref, hi_out, lo_out, sems
+):
+    copies = [
+        pltpu.make_async_copy(hi_hbm, hi_out, sems.at[0]),
+        pltpu.make_async_copy(lo_hbm, lo_out, sems.at[1]),
+    ]
+    for copy in copies:
+        copy.start()
     degrees = iota(beam_ref.shape, 1)
-    for g in range(weight_ref.shape[0]):
+    owned = weight_ref.shape[0]
+    for g in range(owned):
         order = own_ref[g]
         weight_ref[g] = jnp.where(degrees >= order, beam_ref[...], 0.0)
         sign_ref[g] = (1 - 2 * ((degrees + order) & 1)).astype(F32).astype(BF16)
-    owned = weight_ref.shape[0]
     gather_ref[...] = slot_rows(owned, pairs, gather_ref.shape[0] // owned)
+    for copy in copies:
+        copy.wait()
 
 
 def harmonic_kernel(
-    same, pairs, low_pairs, received_ref, weight_ref, sign_ref, gather_ref, hi_hbm, lo_hbm,
-    out_ref, hi_ref, lo_ref, held, sems,
+    same, low_pairs, received_ref, weight_ref, sign_ref, gather_ref, hi_ref, lo_ref, out_ref, held
 ):
     owned, pair_total = hi_ref.shape[:2]
     low_total = lo_ref.shape[1]
     half = received_ref.shape[1] // HEMIS
-    copies = []
-    for g in range(owned):
-        copies.append(
-            [
-                pltpu.make_async_copy(source.at[g], target.at[g], sems.at[k, g])
-                for k, (source, target) in enumerate(((hi_hbm, hi_ref), (lo_hbm, lo_ref)))
-            ]
-        )
-        for copy in copies[g]:
-            copy.start()
     north = dot_tn(received_ref[:, :half], gather_ref[...])
     south = dot_tn(received_ref[:, half:], gather_ref[...])
     for g in range(owned):
         lanes = slice(g * pair_total, (g + 1) * pair_total)
         coeffs = jnp.concatenate([north[:, lanes], south[:, lanes]], axis=1).astype(BF16)
-        for copy in copies[g]:
-            copy.wait()
         hi_table = jnp.concatenate([hi_ref[g], hi_ref[g] * sign_ref[g]], axis=0)
         alm = dot_nn(coeffs, hi_table) * weight_ref[g]
         lo_table = jnp.concatenate([lo_ref[g], lo_ref[g] * sign_ref[g]], axis=0)
-        both = dot_nt(lo_table, jnp.concatenate(split(alm), axis=0))
-        total = (both[:, :half] + both[:, half:]).astype(BF16)
+        both = dot_nt(jnp.concatenate(split(alm), axis=0), lo_table)
+        total = (both[:half] + both[half:]).T.astype(BF16)
         for h in range(HEMIS):
             held[g * low_total : (g + 1) * low_total, h * half : (h + 1) * half] = total[
                 h * low_total : (h + 1) * low_total
@@ -325,30 +322,19 @@
     return jax.ShapeDtypeStruct(shape, dtype)
 
 
-def per_device(
-    sky_maps, hi_cycles, lo_cycles, azimuth_orders, legendre_hi, legendre_lo, beam_weights
-):
-    axes = ("band", "ma")
+def analyse(sky_maps, hi_cycles, azimuth_orders):
     map_count, pairs = sky_maps.shape[:2]
-    low_pairs = lo_cycles.shape[0]
     count = azimuth_orders.shape[0]
-    owned, degree_count, pair_total = legendre_hi.shape
-    low_total = legendre_lo.shape[2]
-    devices = count // owned
-    order_row = azimuth_orders.reshape(1, count)
-    order_column = azimuth_orders.reshape(count, 1)
     cols = HEMIS * 2 * map_count
-
     inner = BF16_ROWS // HEMIS
     blocks = NPIX_HI // (inner * LANES)
     sky = sky_maps.reshape(map_count, pairs, HEMIS, blocks, inner, LANES)
     sky = sky.transpose(0, 1, 3, 4, 2, 5)
     sky = sky.reshape(map_count * pairs, blocks, BF16_ROWS, LANES)
-    quarter = map_count // 4
-    spans = [(k * quarter, quarter) for k in range(3)]
-    spans += [(3 * quarter, quarter // 2), (3 * quarter + quarter // 2, quarter // 2)]
-    raw = pltpu.VMEM((quarter * pairs * BF16_ROWS, 2 * count), F32)
-    outgoing = pl.pallas_call(
+    size = map_count // 4
+    spans = [(k * size, size) for k in range(4)]
+    raw = pltpu.VMEM((size * pairs * BF16_ROWS, 2 * count), F32)
+    return pl.pallas_call(
         functools.partial(analyse_kernel, spans),
         out_shape=struct((count * pairs, cols), BF16),
         in_specs=[hbm(), hbm(), hbm()],
@@ -365,7 +351,24 @@
         ],
         compiler_params=params(),
         name="analyse",
-    )(hi_cycles, order_row, sky)
+    )(hi_cycles, azimuth_orders.reshape(1, count), sky)
+
+
+def per_device(
+    sky_maps, hi_cycles, lo_cycles, azimuth_orders, legendre_hi, legendre_lo, beam_weights
+):
+    axes = ("band", "ma")
+    map_count, pairs = sky_maps.shape[:2]
+    low_pairs = lo_cycles.shape[0]
+    count = azimuth_orders.shape[0]
+    owned, degree_count, pair_total = legendre_hi.shape
+    low_total = legendre_lo.shape[2]
+    devices = count // owned
+    order_row = azimuth_orders.reshape(1, count)
+    order_column = azimuth_orders.reshape(count, 1)
+    cols = HEMIS * 2 * map_count
+
+    outgoing = analyse(sky_maps, hi_cycles, azimuth_orders)
     received = lax.all_to_all(
         outgoing.reshape(devices, owned * pairs, cols), axes, split_axis=0, concat_axis=0, tiled=True
     )
@@ -374,42 +377,34 @@
     own = lax.dynamic_slice_in_dim(azimuth_orders, lax.axis_index(axes) * owned, owned)
     low_rows = count * low_pairs
     same = (low_pairs, low_total) == (pairs, pair_total)
-    weights, signs, gather = pl.pallas_call(
+    hi_blocks, lo_blocks = legendre_hi.transpose(0, 2, 1), legendre_lo.transpose(0, 2, 1)
+    prepared = pl.pallas_call(
         functools.partial(prepare_kernel, pairs),
         out_shape=[
             struct((owned, 1, degree_count), F32),
             struct((owned, 1, degree_count), BF16),
             struct((rows, owned * pair_total), BF16),
+            struct(hi_blocks.shape, BF16),
+            struct(lo_blocks.shape, BF16),
         ],
-        in_specs=[smem(), vmem()],
-        out_specs=[vmem()] * 3,
-        compiler_params=params(16 * 2**20),
+        in_specs=[smem(), vmem(), hbm(), hbm()],
+        out_specs=[vmem()] * 5,
+        scratch_shapes=[pltpu.SemaphoreType.DMA((2,))],
+        compiler_params=params(50 * 2**20),
         cost_estimate=pl.CostEstimate(
             flops=2**10 * degree_count, bytes_accessed=2**10 * degree_count, transcendentals=0
         ),
         name="prepare",
-    )(own, beam_weights.reshape(1, degree_count))
+    )(own, beam_weights.reshape(1, degree_count), hi_blocks, lo_blocks)
     synthesised = pl.pallas_call(
-        functools.partial(harmonic_kernel, same, pairs, low_pairs),
+        functools.partial(harmonic_kernel, same, low_pairs),
         out_shape=struct((low_rows, cols), BF16),
-        in_specs=[vmem(), vmem(), vmem(), vmem(), hbm(), hbm()],
+        in_specs=[vmem()] * 6,
         out_specs=vmem(),
-        scratch_shapes=[
-            pltpu.VMEM((owned, pair_total, degree_count), BF16),
-            pltpu.VMEM((owned, low_total, degree_count), BF16),
-            pltpu.VMEM((owned * low_total, cols), BF16),
-            pltpu.SemaphoreType.DMA((2, owned)),
-        ],
-        compiler_params=params(52 * 2**20),
+        scratch_shapes=[pltpu.VMEM((owned * low_total, cols), BF16)],
+        compiler_params=params(16 * 2**20),
         name="harmonic",
-    )(
-        received.reshape(rows, cols),
-        weights,
-        signs,
-        gather,
-        legendre_hi.transpose(0, 2, 1),
-        legendre_lo.transpose(0, 2, 1),
-    )
+    )(received.reshape(rows, cols), *prepared)
     returned = lax.all_to_all(
         synthesised.reshape(devices, owned * low_pairs, cols),
         axes,

time: 44.2 us -> 38.7 us (0.88)
  Pallas kernels: 20.1 us -> 16.2 us
  waiting for transfers between devices: 12.3 us -> 10.6 us
    pallas_call x2, Pallas kernels: 15.2 us -> 9.66 us  [the longest x1 5.74 us: analyse(): pl.pallas_call(functools.partial(analyse_kernel, spans), out_shape=struct...]
    pallas_call x1, Pallas kernels: 0.72 us -> 2.44 us  [per_device(): pl.pallas_call(functools.partial(prepare_kernel, pairs), out_shape=[struc...]
    all_to_all x1, waiting for transfers between devices: 5.63 us -> 3.92 us  [per_device(): lax.all_to_all(outgoing.reshape(devices, owned * pairs, cols), axes, spli...]
  transfers between devices with their start and end apart: 2 -> 2, of which waited for: 2 -> 2; matrix products, arithmetic and copies ran while one was open for 2% -> 2% of each run, Pallas kernels for 4% -> 9%
where the time goes in v4:
time: 38.7 us; the launch traced here: 38.3 us
  Pallas kernels  16.2 us (42%)
  waiting for transfers between devices  10.6 us (27%)
  starting transfers between devices  9.91 us (26%)
  local copies, waits for them, and re-layouts  1.56 us (4%)
    all_to_all x1, starting transfers between devices, per_device(): lax.all_to_all(outgoing.reshape(devices, owned * pairs, cols), axes, spli...  7.33 us
    all_to_all x1, waiting for transfers between devices, per_device(): lax.all_to_all(synthesised.reshape(devices, owned * low_pairs, cols), axe...  6.66 us
    pallas_call x1, Pallas kernels, analyse(): pl.pallas_call(functools.partial(analyse_kernel, spans), out_shape=struct...  5.74 us
    pallas_call x1, Pallas kernels, per_device(): pl.pallas_call(functools.partial(harmonic_kernel, same, low_pairs), out_s...  3.92 us
    all_to_all x1, waiting for transfers between devices, per_device(): lax.all_to_all(outgoing.reshape(devices, owned * pairs, cols), axes, spli...  3.92 us
    pallas_call x1, Pallas kernels, per_device(): pl.pallas_call(synthesise_kernel, out_shape=struct((map_count, low_pairs,...  3.13 us
    all_to_all x1, starting transfers between devices, per_device(): lax.all_to_all(synthesised.reshape(devices, owned * low_pairs, cols), axe...  2.58 us
    pallas_call x1, Pallas kernels, per_device(): pl.pallas_call(functools.partial(prepare_kernel, pairs), out_shape=[struc...  2.44 us
  transfers between devices with their start and end apart: 2, of which 2 were waited for; matrix products, arithmetic and copies ran while one was open for 2% of the time, Pallas kernels for 9%

profile of v4, /device:TPU:0, one launch (start us, length us, event | category | flops | bytes accessed | tf_op | source)
XLA Modules:
  0.0 38.3 jit_solution(5096748595142785230)
XLA Ops:
  0.0 5.7 %analyse.1 = bf16[256,256]{1,0:T(8,128)(2,1)} custom-call(s32[2]{0:T(128)} %hi_hbm.1, s32[1,128]{1,0:T(1,128)} %bitcast.22, bf16[128,16,16,128]{3,2,1,0:T(8,128)(2,1)} %bitcast.25), custom_call_target="tpu_custom_call" | custom-call | tf_op jit(solution)/shard_map/analyse/pallas_call | solution.py:337
  5.7 7.3 %all-to-all-start = ((bf16[32,8,256]{2,1,0:T(8,128)(2,1)}), bf16[32,8,256]{2,1,0:T(8,128)(2,1)S(1)}, u32[]{:S(2)}, u32[]{:S(2)}) async-start(bf16[32,8,256]{2,1,0:T(8,128)(2,1)} %bitcast.28), calls=%async_computation | async-start | bytes 262144 | tf_op jit(solution)/shard_map/all_to_all | solution.py:372
  13.1 0.7 %dynamic_slice.3.own_ref = s32[4]{0:T(128)S(1)} dynamic-slice(s32[128]{0:T(128)} %param.10, s32[]{:T(128)S(6)} %select_n.3), dynamic_slice_sizes={4} | dynamic-slice | bytes 36 | tf_op jit(solution)/shard_map/dynamic_slice | solution.py:377
  13.8 0.0 copy-start
  13.8 0.7 %copy-done = f32[3072]{0:T(1024)S(1)} copy-done((f32[3072]{0:T(1024)S(1)}, f32[3072]{0:T(1024)}, u32[]{:S(2)}) %copy-start) | copy-done | bytes 12312
  14.5 2.4 %prepare.1 = (f32[4,1,3072]{2,1,0:T(1,128)S(1)}, bf16[4,1,3072]{2,1,0:T(2,128)(2,1)S(1)}, bf16[256,256]{1,0:T(8,128)(2,1)S(1)}, bf16[4,64,3072]{2,1,0:T(8,128)(2,1)S(1)}, bf16[4,64,3072]{2,1,0:T(8,128)(2,1)S(1)}) custom-call(s32[4]{0:T(128)S(1)} %dynamic_slice.3.own_ref, f32[1,3072]{1,0:T(1,128)S(1)} %bitcast.21, bf16[4,64,3072]{2,1,0:T(8,128)(2,1)} %bitcast.26, ...), custom_call_target="tpu_custom_call" | custom-call | flops 3145728 | bytes 3145728 | tf_op jit(solution)/shard_map/prepare/pallas_call | solution.py:381
  17.0 3.9 %all-to-all-done = bf16[32,8,256]{2,1,0:T(8,128)(2,1)S(1)} async-done(((bf16[32,8,256]{2,1,0:T(8,128)(2,1)}), bf16[32,8,256]{2,1,0:T(8,128)(2,1)S(1)}, u32[]{:S(2)}, u32[]{:S(2)}) %all-to-all-start) | async-done | bytes 131104 | tf_op jit(solution)/shard_map/all_to_all | solution.py:372
  20.9 0.0 copy-start.1
  20.9 0.0 copy-start.2
  20.9 3.9 %harmonic.1 = bf16[256,256]{1,0:T(8,128)(2,1)} custom-call(bf16[256,256]{1,0:T(8,128)(2,1)S(1)} %bitcast.19, f32[4,1,3072]{2,1,0:T(1,128)S(1)} %get-tuple-element.16.weight_ref, bf16[4,1,3072]{2,1,0:T(2,128)(2,1)S(1)} %get-tuple-element.17.sign_ref, bf16[256,256]{1,0:T(8,128)(2,1)S(1)} %get-tuple-element.18.gather_ref, ...), custom_call_target="tpu_custom_call" | custom-call | tf_op jit(solution)/shard_map/harmonic/pallas_call | solution.py:399
  24.8 2.6 %all-to-all-start.1 = ((bf16[32,8,256]{2,1,0:T(8,128)(2,1)}), bf16[32,8,256]{2,1,0:T(8,128)(2,1)S(1)}, u32[]{:S(2)}, u32[]{:S(2)}) async-start(bf16[32,8,256]{2,1,0:T(8,128)(2,1)} %bitcast.10), calls=%async_computation.1 | async-start | bytes 262144 | tf_op jit(solution)/shard_map/all_to_all | solution.py:408
  27.4 0.0 copy-done.1
  27.4 0.1 copy.8.column_ref
  27.5 0.0 copy-done.2
  27.5 1.0 %inverse_table.1 = (bf16[256,1024]{1,0:T(8,128)(2,1)S(1)}, bf16[256,256]{1,0:T(8,128)(2,1)S(1)}, f32[2,2,8,128]{3,2,1,0:T(8,128)S(1)}) custom-call(s32[2]{0:T(128)S(1)} %copy-done.2, s32[1,128]{1,0:T(1,128)S(1)} %bitcast.24, s32[128,1]{1,0:T(8,128)S(1)} %copy.8.column_ref), custom_call_target="tpu_custom_call" | custom-call | flops 8388608 | bytes 1048576 | tf_op jit(solution)/shard_map/inverse_table/pallas_call | solution.py:418
  28.5 6.7 %all-to-all-done.1 = bf16[32,8,256]{2,1,0:T(8,128)(2,1)S(1)} async-done(((bf16[32,8,256]{2,1,0:T(8,128)(2,1)}), bf16[32,8,256]{2,1,0:T(8,128)(2,1)S(1)}, u32[]{:S(2)}, u32[]{:S(2)}) %all-to-all-start.1) | async-done | bytes 131104 | tf_op jit(solution)/shard_map/all_to_all | solution.py:408
  35.2 3.1 %synthesise.1 = f32[64,2,8,8,128]{4,3,2,1,0:T(8,128)} custom-call(f32[2,2,8,128]{3,2,1,0:T(8,128)S(1)} %get-tuple-element.13.phase_ref, bf16[256,1024]{1,0:T(8,128)(2,1)S(1)} %get-tuple-element.14.table_ref, bf16[256,256]{1,0:T(8,128)(2,1)S(1)} %get-tuple-element.15.gather_ref, bf16[256,256]{1,0:T(8,128)(2,1)S(1)} %bitcast.20), custom_call_target="tpu_custom_call" | custom-call | tf_op jit(solution)/shard_map/synthesise/pallas_call | solution.py:439
Async XLA Ops:
  5.7 15.1 %all-to-all-start = ((bf16[32,8,256]{2,1,0:T(8,128)(2,1)}), bf16[32,8,256]{2,1,0:T(8,128)(2,1)S(1)}, u32[]{:S(2)}, u32[]{:S(2)}) async-start(bf16[32,8,256]{2,1,0:T(8,128)(2,1)} %bitcast.28), calls=%async_computation | async-start | bytes 262144 | tf_op jit(solution)/shard_map/all_to_all | solution.py:372
  13.8 0.7 %copy-start = (f32[3072]{0:T(1024)S(1)}, f32[3072]{0:T(1024)}, u32[]{:S(2)}) copy-start(f32[3072]{0:T(1024)} %param.13) | copy-start | bytes 36868
  20.9 6.5 %copy-start.1 = (s32[128]{0:T(128)S(1)}, s32[128]{0:T(128)}, u32[]{:S(2)}) copy-start(s32[128]{0:T(128)} %param.10) | copy-start | bytes 1540
  20.9 6.6 %copy-start.2 = (s32[2]{0:T(128)S(1)}, s32[2]{0:T(128)}, u32[]{:S(2)}) copy-start(s32[2]{0:T(128)} %lo_ref.1) | copy-start | bytes 28
  24.8 10.4 %all-to-all-start.1 = ((bf16[32,8,256]{2,1,0:T(8,128)(2,1)}), bf16[32,8,256]{2,1,0:T(8,128)(2,1)S(1)}, u32[]{:S(2)}, u32[]{:S(2)}) async-start(bf16[32,8,256]{2,1,0:T(8,128)(2,1)} %bitcast.10), calls=%async_computation.1 | async-start | bytes 262144 | tf_op jit(solution)/shard_map/all_to_all | solution.py:408

commit v5 on v4

--- a/solution.py
+++ b/solution.py
@@ -256,11 +256,9 @@
 
 
 def synthesise_kernel(
-    phase_ref, table_ref, gather_ref, returned_ref, out_hbm,
-    spectra, high, low, buf_a, buf_b, buf_c, buf_d, sems,
-):
-    buffers = (buf_a, buf_b, buf_c, buf_d)
-    map_count, pairs, wide = buf_a.shape[:3]
+    phase_ref, table_ref, gather_ref, returned_ref, out_hbm, spectra, high, low, buffer, sems
+):
+    pairs, steps, map_count, wide = buffer.shape[:4]
     count = phase_ref.shape[3]
     for j in range(count // LANES):
         rows = slice(j * LANES * pairs, (j + 1) * LANES * pairs)
@@ -269,35 +267,40 @@
             spectra[p, :, j * LANES : (j + 1) * LANES] = turned[:, p * LANES : (p + 1) * LANES]
 
     south = (iota((F32_ROWS, count), 0) & 1) == 1
-    for p in range(pairs):
+
+    def turn(p, i):
+        def spread(c):
+            north = spectra[p, c * map_count + i : c * map_count + i + 1]
+            at = (2 + c) * map_count + i
+            return jnp.where(south, spectra[p, at : at + 1], north)
+
+        real, imag = spread(0), spread(1)
         cosine, sine = phase_ref[p, 0], phase_ref[p, 1]
-
-        def turn(i):
-            def spread(c):
-                north = spectra[p, c * map_count + i : c * map_count + i + 1]
-                at = (2 + c) * map_count + i
-                return jnp.where(south, spectra[p, at : at + 1], north)
-
-            real, imag = spread(0), spread(1)
-            return real * cosine - imag * sine, imag * cosine + real * sine
-
-        for i in range(0, map_count, 2):
+        return real * cosine - imag * sine, imag * cosine + real * sine
+
+    def rotate(p, first, last):
+        for i in range(first, last, 2):
             at = slice((p * map_count + i) * F32_ROWS, (p * map_count + i + 2) * F32_ROWS)
-            for c, parts in enumerate(zip(turn(i), turn(i + 1))):
+            for c, parts in enumerate(zip(turn(p, i), turn(p, i + 1))):
                 lanes = slice(c * count, (c + 1) * count)
                 high[at, lanes], low[at, lanes] = split(jnp.concatenate(parts, axis=0))
 
     copies = []
-    for n, buffer in enumerate(buffers):
-        table = table_ref[:, n * wide * LANES : (n + 1) * wide * LANES]
-        pixels = dot_nn(high[...], table) + dot_nn(low[...], table)
-        pixels = pixels.reshape(pairs, map_count, F32_ROWS, wide * LANES)
-        for p in range(pairs):
+    rotate(0, 0, map_count)
+    for p in range(pairs):
+        rows = slice(p * map_count * F32_ROWS, (p + 1) * map_count * F32_ROWS)
+        for n in range(steps):
+            table = table_ref[:, n * wide * LANES : (n + 1) * wide * LANES]
+            pixels = dot_nn(high[rows], table) + dot_nn(low[rows], table)
+            if p + 1 < pairs:
+                share = map_count // steps
+                rotate(p + 1, n * share, (n + 1) * share)
+            pixels = pixels.reshape(map_count, F32_ROWS, wide * LANES)
             for a in range(wide):
-                buffer[:, p, a] = pixels[p, :, :, a * LANES : (a + 1) * LANES]
-        target = out_hbm.at[:, :, pl.ds(n * wide, wide)]
-        copies.append(pltpu.make_async_copy(buffer, target, sems.at[n]))
-        copies[-1].start()
+                buffer[p, n, :, a] = pixels[:, :, a * LANES : (a + 1) * LANES]
+            target = out_hbm.at[:, p, pl.ds(n * wide, wide)]
+            copies.append(pltpu.make_async_copy(buffer.at[p, n], target, sems.at[p, n]))
+            copies[-1].start()
     for copy in copies:
         copy.wait()
 
@@ -432,9 +435,9 @@
         ),
         name="inverse_table",
     )(lo_cycles, order_row, order_column)
-    steps = 4
+    steps = 2
     wide = blocks_lo // steps
-    buffer = pltpu.VMEM((map_count, low_pairs, wide, F32_ROWS, LANES), F32)
+    buffer = pltpu.VMEM((low_pairs, steps, map_count, wide, F32_ROWS, LANES), F32)
     spectrum = pltpu.VMEM((map_count * low_pairs * F32_ROWS, 2 * count), BF16)
     pixels = pl.pallas_call(
         synthesise_kernel,
@@ -446,10 +449,7 @@
             spectrum,
             spectrum,
             buffer,
-            buffer,
-            buffer,
-            buffer,
-            pltpu.SemaphoreType.DMA((steps,)),
+            pltpu.SemaphoreType.DMA((low_pairs, steps)),
         ],
         compiler_params=params(32 * 2**20),
         name="synthesise",

time: 38.7 us -> 38.4 us (level)
  no operation moved by 1% of the time
where the time goes in v5:
time: 38.4 us; the launch traced here: 38 us
  Pallas kernels  16 us (42%)
  waiting for transfers between devices  10.6 us (28%)
  starting transfers between devices  9.91 us (26%)
  local copies, waits for them, and re-layouts  1.56 us (4%)
    all_to_all x1, starting transfers between devices, per_device(): lax.all_to_all(outgoing.reshape(devices, owned * pairs, cols), axes, spli...  7.33 us
    all_to_all x1, waiting for transfers between devices, per_device(): lax.all_to_all(synthesised.reshape(devices, owned * low_pairs, cols), axe...  6.66 us
    pallas_call x1, Pallas kernels, analyse(): pl.pallas_call(functools.partial(analyse_kernel, spans), out_shape=struct...  5.74 us
    pallas_call x1, Pallas kernels, per_device(): pl.pallas_call(functools.partial(harmonic_kernel, same, low_pairs), out_s...  3.92 us
    all_to_all x1, waiting for transfers between devices, per_device(): lax.all_to_all(outgoing.reshape(devices, owned * pairs, cols), axes, spli...  3.92 us
    pallas_call x1, Pallas kernels, per_device(): pl.pallas_call(synthesise_kernel, out_shape=struct((map_count, low_pairs,...  2.84 us
    all_to_all x1, starting transfers between devices, per_device(): lax.all_to_all(synthesised.reshape(devices, owned * low_pairs, cols), axe...  2.58 us
    pallas_call x1, Pallas kernels, per_device(): pl.pallas_call(functools.partial(prepare_kernel, pairs), out_shape=[struc...  2.44 us
  transfers between devices with their start and end apart: 2, of which 2 were waited for; matrix products, arithmetic and copies ran while one was open for 2% of the time, Pallas kernels for 9%

profile of v5, /device:TPU:0, one launch (start us, length us, event | category | flops | bytes accessed | tf_op | source)
XLA Modules:
  0.0 38.0 jit_solution(14665752339138456030)
XLA Ops:
  0.0 5.7 %analyse.1 = bf16[256,256]{1,0:T(8,128)(2,1)} custom-call(s32[2]{0:T(128)} %hi_hbm.1, s32[1,128]{1,0:T(1,128)} %bitcast.22, bf16[128,16,16,128]{3,2,1,0:T(8,128)(2,1)} %bitcast.25), custom_call_target="tpu_custom_call" | custom-call | tf_op jit(solution)/shard_map/analyse/pallas_call | solution.py:340
  5.7 7.3 %all-to-all-start = ((bf16[32,8,256]{2,1,0:T(8,128)(2,1)}), bf16[32,8,256]{2,1,0:T(8,128)(2,1)S(1)}, u32[]{:S(2)}, u32[]{:S(2)}) async-start(bf16[32,8,256]{2,1,0:T(8,128)(2,1)} %bitcast.28), calls=%async_computation | async-start | bytes 262144 | tf_op jit(solution)/shard_map/all_to_all | solution.py:375
  13.1 0.7 %dynamic_slice.3.own_ref = s32[4]{0:T(128)S(1)} dynamic-slice(s32[128]{0:T(128)} %param.10, s32[]{:T(128)S(6)} %select_n.3), dynamic_slice_sizes={4} | dynamic-slice | bytes 36 | tf_op jit(solution)/shard_map/dynamic_slice | solution.py:380
  13.8 0.0 copy-start
  13.8 0.7 %copy-done = f32[3072]{0:T(1024)S(1)} copy-done((f32[3072]{0:T(1024)S(1)}, f32[3072]{0:T(1024)}, u32[]{:S(2)}) %copy-start) | copy-done | bytes 12312
  14.5 2.4 %prepare.1 = (f32[4,1,3072]{2,1,0:T(1,128)S(1)}, bf16[4,1,3072]{2,1,0:T(2,128)(2,1)S(1)}, bf16[256,256]{1,0:T(8,128)(2,1)S(1)}, bf16[4,64,3072]{2,1,0:T(8,128)(2,1)S(1)}, bf16[4,64,3072]{2,1,0:T(8,128)(2,1)S(1)}) custom-call(s32[4]{0:T(128)S(1)} %dynamic_slice.3.own_ref, f32[1,3072]{1,0:T(1,128)S(1)} %bitcast.21, bf16[4,64,3072]{2,1,0:T(8,128)(2,1)} %bitcast.26, ...), custom_call_target="tpu_custom_call" | custom-call | flops 3145728 | bytes 3145728 | tf_op jit(solution)/shard_map/prepare/pallas_call | solution.py:384
  17.0 3.9 %all-to-all-done = bf16[32,8,256]{2,1,0:T(8,128)(2,1)S(1)} async-done(((bf16[32,8,256]{2,1,0:T(8,128)(2,1)}), bf16[32,8,256]{2,1,0:T(8,128)(2,1)S(1)}, u32[]{:S(2)}, u32[]{:S(2)}) %all-to-all-start) | async-done | bytes 131104 | tf_op jit(solution)/shard_map/all_to_all | solution.py:375
  20.9 0.0 copy-start.1
  20.9 0.0 copy-start.2
  20.9 3.9 %harmonic.1 = bf16[256,256]{1,0:T(8,128)(2,1)} custom-call(bf16[256,256]{1,0:T(8,128)(2,1)S(1)} %bitcast.19, f32[4,1,3072]{2,1,0:T(1,128)S(1)} %get-tuple-element.16.weight_ref, bf16[4,1,3072]{2,1,0:T(2,128)(2,1)S(1)} %get-tuple-element.17.sign_ref, bf16[256,256]{1,0:T(8,128)(2,1)S(1)} %get-tuple-element.18.gather_ref, ...), custom_call_target="tpu_custom_call" | custom-call | tf_op jit(solution)/shard_map/harmonic/pallas_call | solution.py:402
  24.8 2.6 %all-to-all-start.1 = ((bf16[32,8,256]{2,1,0:T(8,128)(2,1)}), bf16[32,8,256]{2,1,0:T(8,128)(2,1)S(1)}, u32[]{:S(2)}, u32[]{:S(2)}) async-start(bf16[32,8,256]{2,1,0:T(8,128)(2,1)} %bitcast.10), calls=%async_computation.1 | async-start | bytes 262144 | tf_op jit(solution)/shard_map/all_to_all | solution.py:411
  27.4 0.0 copy-done.1
  27.4 0.1 copy.8.column_ref
  27.5 0.0 copy-done.2
  27.5 1.0 %inverse_table.1 = (bf16[256,1024]{1,0:T(8,128)(2,1)S(1)}, bf16[256,256]{1,0:T(8,128)(2,1)S(1)}, f32[2,2,8,128]{3,2,1,0:T(8,128)S(1)}) custom-call(s32[2]{0:T(128)S(1)} %copy-done.2, s32[1,128]{1,0:T(1,128)S(1)} %bitcast.24, s32[128,1]{1,0:T(8,128)S(1)} %copy.8.column_ref), custom_call_target="tpu_custom_call" | custom-call | flops 8388608 | bytes 1048576 | tf_op jit(solution)/shard_map/inverse_table/pallas_call | solution.py:421
  28.5 6.7 %all-to-all-done.1 = bf16[32,8,256]{2,1,0:T(8,128)(2,1)S(1)} async-done(((bf16[32,8,256]{2,1,0:T(8,128)(2,1)}), bf16[32,8,256]{2,1,0:T(8,128)(2,1)S(1)}, u32[]{:S(2)}, u32[]{:S(2)}) %all-to-all-start.1) | async-done | bytes 131104 | tf_op jit(solution)/shard_map/all_to_all | solution.py:411
  35.2 2.8 %synthesise.1 = f32[64,2,8,8,128]{4,3,2,1,0:T(8,128)} custom-call(f32[2,2,8,128]{3,2,1,0:T(8,128)S(1)} %get-tuple-element.13.phase_ref, bf16[256,1024]{1,0:T(8,128)(2,1)S(1)} %get-tuple-element.14.table_ref, bf16[256,256]{1,0:T(8,128)(2,1)S(1)} %get-tuple-element.15.gather_ref, bf16[256,256]{1,0:T(8,128)(2,1)S(1)} %bitcast.20), custom_call_target="tpu_custom_call" | custom-call | tf_op jit(solution)/shard_map/synthesise/pallas_call | solution.py:442
Async XLA Ops:
  5.7 15.1 %all-to-all-start = ((bf16[32,8,256]{2,1,0:T(8,128)(2,1)}), bf16[32,8,256]{2,1,0:T(8,128)(2,1)S(1)}, u32[]{:S(2)}, u32[]{:S(2)}) async-start(bf16[32,8,256]{2,1,0:T(8,128)(2,1)} %bitcast.28), calls=%async_computation | async-start | bytes 262144 | tf_op jit(solution)/shard_map/all_to_all | solution.py:375
  13.8 0.7 %copy-start = (f32[3072]{0:T(1024)S(1)}, f32[3072]{0:T(1024)}, u32[]{:S(2)}) copy-start(f32[3072]{0:T(1024)} %param.13) | copy-start | bytes 36868
  20.9 6.5 %copy-start.1 = (s32[128]{0:T(128)S(1)}, s32[128]{0:T(128)}, u32[]{:S(2)}) copy-start(s32[128]{0:T(128)} %param.10) | copy-start | bytes 1540
  20.9 6.6 %copy-start.2 = (s32[2]{0:T(128)S(1)}, s32[2]{0:T(128)}, u32[]{:S(2)}) copy-start(s32[2]{0:T(128)} %lo_ref.1) | copy-start | bytes 28
  24.8 10.4 %all-to-all-start.1 = ((bf16[32,8,256]{2,1,0:T(8,128)(2,1)}), bf16[32,8,256]{2,1,0:T(8,128)(2,1)S(1)}, u32[]{:S(2)}, u32[]{:S(2)}) async-start(bf16[32,8,256]{2,1,0:T(8,128)(2,1)} %bitcast.10), calls=%async_computation.1 | async-start | bytes 262144 | tf_op jit(solution)/shard_map/all_to_all | solution.py:411

commit v6 on v5

--- a/solution.py
+++ b/solution.py
@@ -175,7 +175,7 @@
 
 
 def inverse_table_kernel(
-    pairs, lo_ref, orders_ref, column_ref, table_ref, gather_ref, phase_ref
+    pairs, lo_ref, orders_ref, column_ref, table_ref, residue_ref, gather_ref, phase_ref
 ):
     count = column_ref.shape[0]
     orders = orders_ref[...]
@@ -194,8 +194,8 @@
     )
     for a in range(table_ref.shape[1] // LANES):
         lanes = slice(a * LANES, (a + 1) * LANES)
-        table_ref[:count, lanes] = cosine.astype(BF16)
-        table_ref[count:, lanes] = (-sine).astype(BF16)
+        table_ref[:count, lanes], residue_ref[:count, lanes] = split(cosine)
+        table_ref[count:, lanes], residue_ref[count:, lanes] = split(-sine)
         cosine, sine = (
             cosine * cos_step - sine * sin_step,
             sine * cos_step + cosine * sin_step,
@@ -245,8 +245,7 @@
         hi_table = jnp.concatenate([hi_ref[g], hi_ref[g] * sign_ref[g]], axis=0)
         alm = dot_nn(coeffs, hi_table) * weight_ref[g]
         lo_table = jnp.concatenate([lo_ref[g], lo_ref[g] * sign_ref[g]], axis=0)
-        both = dot_nt(jnp.concatenate(split(alm), axis=0), lo_table)
-        total = (both[:half] + both[half:]).T.astype(BF16)
+        total = dot_nt(lo_table, alm.astype(BF16)).astype(BF16)
         for h in range(HEMIS):
             held[g * low_total : (g + 1) * low_total, h * half : (h + 1) * half] = total[
                 h * low_total : (h + 1) * low_total
@@ -256,7 +255,8 @@
 
 
 def synthesise_kernel(
-    phase_ref, table_ref, gather_ref, returned_ref, out_hbm, spectra, high, low, buffer, sems
+    phase_ref, table_ref, residue_ref, gather_ref, returned_ref, out_hbm,
+    spectra, high, low, buffer, sems,
 ):
     pairs, steps, map_count, wide = buffer.shape[:4]
     count = phase_ref.shape[3]
@@ -290,8 +290,9 @@
     for p in range(pairs):
         rows = slice(p * map_count * F32_ROWS, (p + 1) * map_count * F32_ROWS)
         for n in range(steps):
-            table = table_ref[:, n * wide * LANES : (n + 1) * wide * LANES]
-            pixels = dot_nn(high[rows], table) + dot_nn(low[rows], table)
+            lanes = slice(n * wide * LANES, (n + 1) * wide * LANES)
+            pixels = dot_nn(high[rows], table_ref[:, lanes]) + dot_nn(low[rows], table_ref[:, lanes])
+            pixels += dot_nn(high[rows], residue_ref[:, lanes])
             if p + 1 < pairs:
                 share = map_count // steps
                 rotate(p + 1, n * share, (n + 1) * share)
@@ -418,15 +419,16 @@
 
     blocks_lo = NPIX_LO // (F32_ROWS // HEMIS * LANES)
     side = LANES * low_pairs
-    inverse_table, regroup, phase = pl.pallas_call(
+    inverse_table, residue, regroup, phase = pl.pallas_call(
         functools.partial(inverse_table_kernel, low_pairs),
         out_shape=[
+            struct((2 * count, blocks_lo * LANES), BF16),
             struct((2 * count, blocks_lo * LANES), BF16),
             struct((side, side), BF16),
             struct((low_pairs, 2, F32_ROWS, count), F32),
         ],
         in_specs=[smem(), vmem(), vmem()],
-        out_specs=[vmem()] * 3,
+        out_specs=[vmem()] * 4,
         compiler_params=params(8 * 2**20),
         cost_estimate=pl.CostEstimate(
             flops=64 * count * blocks_lo * LANES,
@@ -442,7 +444,7 @@
     pixels = pl.pallas_call(
         synthesise_kernel,
         out_shape=struct((map_count, low_pairs, blocks_lo, F32_ROWS, LANES), F32),
-        in_specs=[vmem(), vmem(), vmem(), vmem()],
+        in_specs=[vmem()] * 5,
         out_specs=hbm(),
         scratch_shapes=[
             pltpu.VMEM((low_pairs, cols, count), F32),
@@ -453,7 +455,7 @@
         ],
         compiler_params=params(32 * 2**20),
         name="synthesise",
-    )(phase, inverse_table, regroup, returned.reshape(low_rows, cols))
+    )(phase, inverse_table, residue, regroup, returned.reshape(low_rows, cols))
     pixels = pixels.reshape(map_count, low_pairs, blocks_lo, F32_ROWS // HEMIS, HEMIS, LANES)
     pixels = pixels.transpose(0, 1, 4, 2, 3, 5)
     return pixels.reshape(map_count, low_pairs, HEMIS, NPIX_LO)

time: 38.4 us -> 37.9 us (0.987)
  waiting for transfers between devices: 10.6 us -> 10.2 us
    pallas_call x1, Pallas kernels: 3.92 us -> 3.06 us  [per_device(): pl.pallas_call(functools.partial(harmonic_kernel, same, low_pairs), out_s...]
  transfers between devices with their start and end apart: 2 -> 2, of which waited for: 2 -> 2; matrix products, arithmetic and copies ran while one was open for 2% -> 2% of each run, Pallas kernels for 9% -> 10%
where the time goes in v6:
time: 37.9 us; the launch traced here: 37.5 us
  Pallas kernels  15.7 us (41%)
  waiting for transfers between devices  10.2 us (27%)
  starting transfers between devices  9.91 us (26%)
  local copies, waits for them, and re-layouts  1.56 us (4%)
    all_to_all x1, starting transfers between devices, per_device(): lax.all_to_all(outgoing.reshape(devices, owned * pairs, cols), axes, spli...  7.33 us
    all_to_all x1, waiting for transfers between devices, per_device(): lax.all_to_all(synthesised.reshape(devices, owned * low_pairs, cols), axe...  6.32 us
    pallas_call x1, Pallas kernels, analyse(): pl.pallas_call(functools.partial(analyse_kernel, spans), out_shape=struct...  5.74 us
    all_to_all x1, waiting for transfers between devices, per_device(): lax.all_to_all(outgoing.reshape(devices, owned * pairs, cols), axes, spli...  3.92 us
    pallas_call x1, Pallas kernels, per_device(): pl.pallas_call(synthesise_kernel, out_shape=struct((map_count, low_pairs,...  3.14 us
    pallas_call x1, Pallas kernels, per_device(): pl.pallas_call(functools.partial(harmonic_kernel, same, low_pairs), out_s...  3.06 us
    all_to_all x1, starting transfers between devices, per_device(): lax.all_to_all(synthesised.reshape(devices, owned * low_pairs, cols), axe...  2.58 us
    pallas_call x1, Pallas kernels, per_device(): pl.pallas_call(functools.partial(prepare_kernel, pairs), out_shape=[struc...  2.44 us
  transfers between devices with their start and end apart: 2, of which 2 were waited for; matrix products, arithmetic and copies ran while one was open for 2% of the time, Pallas kernels for 10%

profile of v6, /device:TPU:0, one launch (start us, length us, event | category | flops | bytes accessed | tf_op | source)
XLA Modules:
  0.0 37.5 jit_solution(17535913915399801992)
XLA Ops:
  0.0 5.7 %analyse.1 = bf16[256,256]{1,0:T(8,128)(2,1)} custom-call(s32[2]{0:T(128)} %hi_hbm.1, s32[1,128]{1,0:T(1,128)} %bitcast.22, bf16[128,16,16,128]{3,2,1,0:T(8,128)(2,1)} %bitcast.25), custom_call_target="tpu_custom_call" | custom-call | tf_op jit(solution)/shard_map/analyse/pallas_call | solution.py:341
  5.7 7.3 %all-to-all-start = ((bf16[32,8,256]{2,1,0:T(8,128)(2,1)}), bf16[32,8,256]{2,1,0:T(8,128)(2,1)S(1)}, u32[]{:S(2)}, u32[]{:S(2)}) async-start(bf16[32,8,256]{2,1,0:T(8,128)(2,1)} %bitcast.28), calls=%async_computation | async-start | bytes 262144 | tf_op jit(solution)/shard_map/all_to_all | solution.py:376
  13.1 0.7 %dynamic_slice.3.own_ref = s32[4]{0:T(128)S(1)} dynamic-slice(s32[128]{0:T(128)} %param.10, s32[]{:T(128)S(6)} %select_n.3), dynamic_slice_sizes={4} | dynamic-slice | bytes 36 | tf_op jit(solution)/shard_map/dynamic_slice | solution.py:381
  13.8 0.0 copy-start
  13.8 0.7 %copy-done = f32[3072]{0:T(1024)S(1)} copy-done((f32[3072]{0:T(1024)S(1)}, f32[3072]{0:T(1024)}, u32[]{:S(2)}) %copy-start) | copy-done | bytes 12312
  14.5 2.4 %prepare.1 = (f32[4,1,3072]{2,1,0:T(1,128)S(1)}, bf16[4,1,3072]{2,1,0:T(2,128)(2,1)S(1)}, bf16[256,256]{1,0:T(8,128)(2,1)S(1)}, bf16[4,64,3072]{2,1,0:T(8,128)(2,1)S(1)}, bf16[4,64,3072]{2,1,0:T(8,128)(2,1)S(1)}) custom-call(s32[4]{0:T(128)S(1)} %dynamic_slice.3.own_ref, f32[1,3072]{1,0:T(1,128)S(1)} %bitcast.21, bf16[4,64,3072]{2,1,0:T(8,128)(2,1)} %bitcast.26, ...), custom_call_target="tpu_custom_call" | custom-call | flops 3145728 | bytes 3145728 | tf_op jit(solution)/shard_map/prepare/pallas_call | solution.py:385
  17.0 3.9 %all-to-all-done = bf16[32,8,256]{2,1,0:T(8,128)(2,1)S(1)} async-done(((bf16[32,8,256]{2,1,0:T(8,128)(2,1)}), bf16[32,8,256]{2,1,0:T(8,128)(2,1)S(1)}, u32[]{:S(2)}, u32[]{:S(2)}) %all-to-all-start) | async-done | bytes 131104 | tf_op jit(solution)/shard_map/all_to_all | solution.py:376
  20.9 0.0 copy-start.1
  20.9 0.0 copy-start.2
  20.9 3.1 %harmonic.1 = bf16[256,256]{1,0:T(8,128)(2,1)} custom-call(bf16[256,256]{1,0:T(8,128)(2,1)S(1)} %bitcast.19, f32[4,1,3072]{2,1,0:T(1,128)S(1)} %get-tuple-element.18.weight_ref, bf16[4,1,3072]{2,1,0:T(2,128)(2,1)S(1)} %get-tuple-element.19.sign_ref, bf16[256,256]{1,0:T(8,128)(2,1)S(1)} %get-tuple-element.20.gather_ref, ...), custom_call_target="tpu_custom_call" | custom-call | tf_op jit(solution)/shard_map/harmonic/pallas_call | solution.py:403
  24.0 2.6 %all-to-all-start.1 = ((bf16[32,8,256]{2,1,0:T(8,128)(2,1)}), bf16[32,8,256]{2,1,0:T(8,128)(2,1)S(1)}, u32[]{:S(2)}, u32[]{:S(2)}) async-start(bf16[32,8,256]{2,1,0:T(8,128)(2,1)} %bitcast.10), calls=%async_computation.1 | async-start | bytes 262144 | tf_op jit(solution)/shard_map/all_to_all | solution.py:412
  26.5 0.0 copy-done.1
  26.6 0.1 copy.8.column_ref
  26.7 0.0 copy-done.2
  26.7 1.4 %inverse_table.1 = (bf16[256,1024]{1,0:T(8,128)(2,1)S(1)}, bf16[256,1024]{1,0:T(8,128)(2,1)S(1)}, bf16[256,256]{1,0:T(8,128)(2,1)S(1)}, f32[2,2,8,128]{3,2,1,0:T(8,128)S(1)}) custom-call(s32[2]{0:T(128)S(1)} %copy-done.2, s32[1,128]{1,0:T(1,128)S(1)} %bitcast.24, s32[128,1]{1,0:T(8,128)S(1)} %copy.8.column_ref), custom_call_target="tpu_custom_call" | custom-call | flops 8388608 | bytes 1048576 | tf_op jit(solution)/shard_map/inverse_table/pallas_call | solution.py:422
  28.0 6.3 %all-to-all-done.1 = bf16[32,8,256]{2,1,0:T(8,128)(2,1)S(1)} async-done(((bf16[32,8,256]{2,1,0:T(8,128)(2,1)}), bf16[32,8,256]{2,1,0:T(8,128)(2,1)S(1)}, u32[]{:S(2)}, u32[]{:S(2)}) %all-to-all-start.1) | async-done | bytes 131104 | tf_op jit(solution)/shard_map/all_to_all | solution.py:412
  34.3 3.1 %synthesise.1 = f32[64,2,8,8,128]{4,3,2,1,0:T(8,128)} custom-call(f32[2,2,8,128]{3,2,1,0:T(8,128)S(1)} %get-tuple-element.14.phase_ref, bf16[256,1024]{1,0:T(8,128)(2,1)S(1)} %get-tuple-element.15.table_ref, bf16[256,1024]{1,0:T(8,128)(2,1)S(1)} %get-tuple-element.16.residue_ref, bf16[256,256]{1,0:T(8,128)(2,1)S(1)} %get-tuple-element.17.gather_ref, ...), custom_call_target="tpu_custom_call" | custom-call | tf_op jit(solution)/shard_map/synthesise/pallas_call | solution.py:444
Async XLA Ops:
  5.7 15.1 %all-to-all-start = ((bf16[32,8,256]{2,1,0:T(8,128)(2,1)}), bf16[32,8,256]{2,1,0:T(8,128)(2,1)S(1)}, u32[]{:S(2)}, u32[]{:S(2)}) async-start(bf16[32,8,256]{2,1,0:T(8,128)(2,1)} %bitcast.28), calls=%async_computation | async-start | bytes 262144 | tf_op jit(solution)/shard_map/all_to_all | solution.py:376
  13.8 0.7 %copy-start = (f32[3072]{0:T(1024)S(1)}, f32[3072]{0:T(1024)}, u32[]{:S(2)}) copy-start(f32[3072]{0:T(1024)} %param.13) | copy-start | bytes 36868
  20.9 5.6 %copy-start.1 = (s32[128]{0:T(128)S(1)}, s32[128]{0:T(128)}, u32[]{:S(2)}) copy-start(s32[128]{0:T(128)} %param.10) | copy-start | bytes 1540
  20.9 5.8 %copy-start.2 = (s32[2]{0:T(128)S(1)}, s32[2]{0:T(128)}, u32[]{:S(2)}) copy-start(s32[2]{0:T(128)} %lo_ref.1) | copy-start | bytes 28
  24.0 10.4 %all-to-all-start.1 = ((bf16[32,8,256]{2,1,0:T(8,128)(2,1)}), bf16[32,8,256]{2,1,0:T(8,128)(2,1)S(1)}, u32[]{:S(2)}, u32[]{:S(2)}) async-start(bf16[32,8,256]{2,1,0:T(8,128)(2,1)} %bitcast.10), calls=%async_computation.1 | async-start | bytes 262144 | tf_op jit(solution)/shard_map/all_to_all | solution.py:412

commit v7 on v6

--- a/solution.py
+++ b/solution.py
@@ -89,8 +89,8 @@
         pltpu.make_async_copy(hi_hbm, hi, sems.at[1]),
     ]
     copies = []
-    for c, (start, size) in enumerate(spans):
-        part = pl.ds(start * pairs, size * pairs)
+    for c, (_, start, size, first, last) in enumerate(spans):
+        part = (pl.ds(start * pairs, size * pairs), pl.ds(first, last - first))
         copies.append(pltpu.make_async_copy(sky_hbm.at[part], sky.at[part], sems.at[2 + c]))
     for copy in small + copies:
         copy.start()
@@ -112,21 +112,22 @@
         cosine, sine = unit_circle(orders * step & (2 * NPIX_HI - 1), 2 * NPIX_HI)
         cos_p.append(cosine * scale)
         sin_p.append(sine * scale)
-    copies[0].wait()
     for a in range(blocks):
         ca, sa = cos_a[a : a + 1], sin_a[a : a + 1]
         table[a * LANES : (a + 1) * LANES, :count] = (ca * cos_l - sa * sin_l).astype(BF16)
         table[a * LANES : (a + 1) * LANES, count:] = (sa * cos_l + ca * sin_l).astype(BF16)
 
     def contract(c):
-        start, size = spans[c]
+        chunk, start, size, first, last = spans[c]
         part = slice(start * pairs, (start + size) * pairs)
+        full = size * pairs * BF16_ROWS
         rows = jnp.concatenate(
-            [sky[part, a].reshape(size * pairs * BF16_ROWS, LANES) for a in range(blocks)], axis=1
+            [sky[part, a].reshape(full, LANES) for a in range(first, last)], axis=1
         )
-        full = size * pairs * BF16_ROWS
-        raws[c % 2][: full // 2] = dot_nn(rows[: full // 2], table[...])
-        raws[c % 2][full // 2 : full] = dot_nn(rows[full // 2 :], table[...])
+        depth = slice(first * LANES, last * LANES)
+        for half in (slice(0, full // 2), slice(full // 2, full)):
+            raw = dot_nn(rows[half], table[depth])
+            raws[chunk % 2][half] = raw if first == 0 else raws[chunk % 2][half] + raw
 
     sub = iota((1, F32_ROWS, count), 1)
 
@@ -145,10 +146,12 @@
         return north[0], south[0]
 
     def finish(c):
-        start, size = spans[c]
+        chunk, start, size, _, last = spans[c]
+        if last < blocks:
+            return
         rows = 8 * pairs * BF16_ROWS
         for group in range(size // 8):
-            raw = raws[c % 2][group * rows : (group + 1) * rows]
+            raw = raws[chunk % 2][group * rows : (group + 1) * rows]
             raw = raw.reshape(8, pairs, BF16_ROWS, 2 * count)
             at = start + group * 8
             for p in range(pairs):
@@ -160,6 +163,7 @@
                     sums[p, h, 0, at : at + 8] = real[h]
                     sums[p, h, 1, at : at + 8] = -imag[h]
 
+    copies[0].wait()
     contract(0)
     for c in range(1, len(spans)):
         copies[c].wait()
@@ -239,13 +243,18 @@
     half = received_ref.shape[1] // HEMIS
     north = dot_tn(received_ref[:, :half], gather_ref[...])
     south = dot_tn(received_ref[:, half:], gather_ref[...])
-    for g in range(owned):
+    def analyse_slot(g):
         lanes = slice(g * pair_total, (g + 1) * pair_total)
         coeffs = jnp.concatenate([north[:, lanes], south[:, lanes]], axis=1).astype(BF16)
         hi_table = jnp.concatenate([hi_ref[g], hi_ref[g] * sign_ref[g]], axis=0)
-        alm = dot_nn(coeffs, hi_table) * weight_ref[g]
+        return (dot_nn(coeffs, hi_table) * weight_ref[g]).astype(BF16)
+
+    alms = [analyse_slot(g) for g in range(1)]
+    for g in range(owned):
+        if g + 1 < owned:
+            alms.append(analyse_slot(g + 1))
         lo_table = jnp.concatenate([lo_ref[g], lo_ref[g] * sign_ref[g]], axis=0)
-        total = dot_nt(lo_table, alm.astype(BF16)).astype(BF16)
+        total = dot_nt(lo_table, alms[g]).astype(BF16)
         for h in range(HEMIS):
             held[g * low_total : (g + 1) * low_total, h * half : (h + 1) * half] = total[
                 h * low_total : (h + 1) * low_total
@@ -336,7 +345,10 @@
     sky = sky.transpose(0, 1, 3, 4, 2, 5)
     sky = sky.reshape(map_count * pairs, blocks, BF16_ROWS, LANES)
     size = map_count // 4
-    spans = [(k * size, size) for k in range(4)]
+    spans = []
+    for k in range(4):
+        edges = (0, blocks // 2, blocks) if k in (0, 3) else (0, blocks)
+        spans += [(k, k * size, size, *edge) for edge in zip(edges, edges[1:])]
     raw = pltpu.VMEM((size * pairs * BF16_ROWS, 2 * count), F32)
     return pl.pallas_call(
         functools.partial(analyse_kernel, spans),

time: 37.9 us -> 37.5 us (0.989)
  no operation moved by 1% of the time
where the time goes in v7:
time: 37.5 us; the launch traced here: 37.2 us
  Pallas kernels  15.4 us (41%)
  waiting for transfers between devices  10.2 us (27%)
  starting transfers between devices  9.91 us (26%)
  local copies, waits for them, and re-layouts  1.56 us (4%)
    all_to_all x1, starting transfers between devices, per_device(): lax.all_to_all(outgoing.reshape(devices, owned * pairs, cols), axes, spli...  7.33 us
    all_to_all x1, waiting for transfers between devices, per_device(): lax.all_to_all(synthesised.reshape(devices, owned * low_pairs, cols), axe...  6.32 us
    pallas_call x1, Pallas kernels, analyse(): pl.pallas_call(functools.partial(analyse_kernel, spans), out_shape=struct...  5.56 us
    all_to_all x1, waiting for transfers between devices, per_device(): lax.all_to_all(outgoing.reshape(devices, owned * pairs, cols), axes, spli...  3.92 us
    pallas_call x1, Pallas kernels, per_device(): pl.pallas_call(synthesise_kernel, out_shape=struct((map_count, low_pairs,...  3.14 us
    pallas_call x1, Pallas kernels, per_device(): pl.pallas_call(functools.partial(harmonic_kernel, same, low_pairs), out_s...  2.91 us
    all_to_all x1, starting transfers between devices, per_device(): lax.all_to_all(synthesised.reshape(devices, owned * low_pairs, cols), axe...  2.58 us
    pallas_call x1, Pallas kernels, per_device(): pl.pallas_call(functools.partial(prepare_kernel, pairs), out_shape=[struc...  2.44 us
  transfers between devices with their start and end apart: 2, of which 2 were waited for; matrix products, arithmetic and copies ran while one was open for 2% of the time, Pallas kernels for 10%

profile of v7, /device:TPU:0, one launch (start us, length us, event | category | flops | bytes accessed | tf_op | source)
XLA Modules:
  0.0 37.2 jit_solution(8622611073858671097)
XLA Ops:
  0.0 5.6 %analyse.1 = bf16[256,256]{1,0:T(8,128)(2,1)} custom-call(s32[2]{0:T(128)} %hi_hbm.1, s32[1,128]{1,0:T(1,128)} %bitcast.22, bf16[128,16,16,128]{3,2,1,0:T(8,128)(2,1)} %bitcast.25), custom_call_target="tpu_custom_call" | custom-call | tf_op jit(solution)/shard_map/analyse/pallas_call | solution.py:353
  5.6 7.3 %all-to-all-start = ((bf16[32,8,256]{2,1,0:T(8,128)(2,1)}), bf16[32,8,256]{2,1,0:T(8,128)(2,1)S(1)}, u32[]{:S(2)}, u32[]{:S(2)}) async-start(bf16[32,8,256]{2,1,0:T(8,128)(2,1)} %bitcast.28), calls=%async_computation | async-start | bytes 262144 | tf_op jit(solution)/shard_map/all_to_all | solution.py:388
  12.9 0.7 %dynamic_slice.3.own_ref = s32[4]{0:T(128)S(1)} dynamic-slice(s32[128]{0:T(128)} %param.10, s32[]{:T(128)S(6)} %select_n.3), dynamic_slice_sizes={4} | dynamic-slice | bytes 36 | tf_op jit(solution)/shard_map/dynamic_slice | solution.py:393
  13.7 0.0 copy-start
  13.7 0.7 %copy-done = f32[3072]{0:T(1024)S(1)} copy-done((f32[3072]{0:T(1024)S(1)}, f32[3072]{0:T(1024)}, u32[]{:S(2)}) %copy-start) | copy-done | bytes 12312
  14.4 2.4 %prepare.1 = (f32[4,1,3072]{2,1,0:T(1,128)S(1)}, bf16[4,1,3072]{2,1,0:T(2,128)(2,1)S(1)}, bf16[256,256]{1,0:T(8,128)(2,1)S(1)}, bf16[4,64,3072]{2,1,0:T(8,128)(2,1)S(1)}, bf16[4,64,3072]{2,1,0:T(8,128)(2,1)S(1)}) custom-call(s32[4]{0:T(128)S(1)} %dynamic_slice.3.own_ref, f32[1,3072]{1,0:T(1,128)S(1)} %bitcast.21, bf16[4,64,3072]{2,1,0:T(8,128)(2,1)} %bitcast.26, ...), custom_call_target="tpu_custom_call" | custom-call | flops 3145728 | bytes 3145728 | tf_op jit(solution)/shard_map/prepare/pallas_call | solution.py:397
  16.8 3.9 %all-to-all-done = bf16[32,8,256]{2,1,0:T(8,128)(2,1)S(1)} async-done(((bf16[32,8,256]{2,1,0:T(8,128)(2,1)}), bf16[32,8,256]{2,1,0:T(8,128)(2,1)S(1)}, u32[]{:S(2)}, u32[]{:S(2)}) %all-to-all-start) | async-done | bytes 131104 | tf_op jit(solution)/shard_map/all_to_all | solution.py:388
  20.7 0.0 copy-start.1
  20.7 0.0 copy-start.2
  20.7 2.9 %harmonic.1 = bf16[256,256]{1,0:T(8,128)(2,1)} custom-call(bf16[256,256]{1,0:T(8,128)(2,1)S(1)} %bitcast.19, f32[4,1,3072]{2,1,0:T(1,128)S(1)} %get-tuple-element.18.weight_ref, bf16[4,1,3072]{2,1,0:T(2,128)(2,1)S(1)} %get-tuple-element.19.sign_ref, bf16[256,256]{1,0:T(8,128)(2,1)S(1)} %get-tuple-element.20.gather_ref, ...), custom_call_target="tpu_custom_call" | custom-call | tf_op jit(solution)/shard_map/harmonic/pallas_call | solution.py:415
  23.6 2.6 %all-to-all-start.1 = ((bf16[32,8,256]{2,1,0:T(8,128)(2,1)}), bf16[32,8,256]{2,1,0:T(8,128)(2,1)S(1)}, u32[]{:S(2)}, u32[]{:S(2)}) async-start(bf16[32,8,256]{2,1,0:T(8,128)(2,1)} %bitcast.10), calls=%async_computation.1 | async-start | bytes 262144 | tf_op jit(solution)/shard_map/all_to_all | solution.py:424
  26.2 0.0 copy-done.1
  26.2 0.1 copy.8.column_ref
  26.3 0.0 copy-done.2
  26.4 1.4 %inverse_table.1 = (bf16[256,1024]{1,0:T(8,128)(2,1)S(1)}, bf16[256,1024]{1,0:T(8,128)(2,1)S(1)}, bf16[256,256]{1,0:T(8,128)(2,1)S(1)}, f32[2,2,8,128]{3,2,1,0:T(8,128)S(1)}) custom-call(s32[2]{0:T(128)S(1)} %copy-done.2, s32[1,128]{1,0:T(1,128)S(1)} %bitcast.24, s32[128,1]{1,0:T(8,128)S(1)} %copy.8.column_ref), custom_call_target="tpu_custom_call" | custom-call | flops 8388608 | bytes 1048576 | tf_op jit(solution)/shard_map/inverse_table/pallas_call | solution.py:434
  27.7 6.3 %all-to-all-done.1 = bf16[32,8,256]{2,1,0:T(8,128)(2,1)S(1)} async-done(((bf16[32,8,256]{2,1,0:T(8,128)(2,1)}), bf16[32,8,256]{2,1,0:T(8,128)(2,1)S(1)}, u32[]{:S(2)}, u32[]{:S(2)}) %all-to-all-start.1) | async-done | bytes 131104 | tf_op jit(solution)/shard_map/all_to_all | solution.py:424
  34.0 3.1 %synthesise.1 = f32[64,2,8,8,128]{4,3,2,1,0:T(8,128)} custom-call(f32[2,2,8,128]{3,2,1,0:T(8,128)S(1)} %get-tuple-element.14.phase_ref, bf16[256,1024]{1,0:T(8,128)(2,1)S(1)} %get-tuple-element.15.table_ref, bf16[256,1024]{1,0:T(8,128)(2,1)S(1)} %get-tuple-element.16.residue_ref, bf16[256,256]{1,0:T(8,128)(2,1)S(1)} %get-tuple-element.17.gather_ref, ...), custom_call_target="tpu_custom_call" | custom-call | tf_op jit(solution)/shard_map/synthesise/pallas_call | solution.py:456
Async XLA Ops:
  5.6 15.1 %all-to-all-start = ((bf16[32,8,256]{2,1,0:T(8,128)(2,1)}), bf16[32,8,256]{2,1,0:T(8,128)(2,1)S(1)}, u32[]{:S(2)}, u32[]{:S(2)}) async-start(bf16[32,8,256]{2,1,0:T(8,128)(2,1)} %bitcast.28), calls=%async_computation | async-start | bytes 262144 | tf_op jit(solution)/shard_map/all_to_all | solution.py:388
  13.7 0.7 %copy-start = (f32[3072]{0:T(1024)S(1)}, f32[3072]{0:T(1024)}, u32[]{:S(2)}) copy-start(f32[3072]{0:T(1024)} %param.13) | copy-start | bytes 36868
  20.7 5.5 %copy-start.1 = (s32[128]{0:T(128)S(1)}, s32[128]{0:T(128)}, u32[]{:S(2)}) copy-start(s32[128]{0:T(128)} %param.10) | copy-start | bytes 1540
  20.7 5.6 %copy-start.2 = (s32[2]{0:T(128)S(1)}, s32[2]{0:T(128)}, u32[]{:S(2)}) copy-start(s32[2]{0:T(128)} %lo_ref.1) | copy-start | bytes 28
  23.6 10.4 %all-to-all-start.1 = ((bf16[32,8,256]{2,1,0:T(8,128)(2,1)}), bf16[32,8,256]{2,1,0:T(8,128)(2,1)S(1)}, u32[]{:S(2)}, u32[]{:S(2)}) async-start(bf16[32,8,256]{2,1,0:T(8,128)(2,1)} %bitcast.10), calls=%async_computation.1 | async-start | bytes 262144 | tf_op jit(solution)/shard_map/all_to_all | solution.py:424

commit v8 on v7

--- a/solution.py
+++ b/solution.py
@@ -347,7 +347,7 @@
     size = map_count // 4
     spans = []
     for k in range(4):
-        edges = (0, blocks // 2, blocks) if k in (0, 3) else (0, blocks)
+        edges = (0, blocks // 2, blocks) if k == 0 else (0, blocks)
         spans += [(k, k * size, size, *edge) for edge in zip(edges, edges[1:])]
     raw = pltpu.VMEM((size * pairs * BF16_ROWS, 2 * count), F32)
     return pl.pallas_call(

time: 37.5 us -> 37.5 us (level)
  no operation moved by 1% of the time
where the time goes in v8:
time: 37.5 us; the launch traced here: 37.2 us
  Pallas kernels  15.4 us (41%)
  waiting for transfers between devices  10.2 us (27%)
  starting transfers between devices  9.91 us (26%)
  local copies, waits for them, and re-layouts  1.56 us (4%)
    all_to_all x1, starting transfers between devices, per_device(): lax.all_to_all(outgoing.reshape(devices, owned * pairs, cols), axes, spli...  7.33 us
    all_to_all x1, waiting for transfers between devices, per_device(): lax.all_to_all(synthesised.reshape(devices, owned * low_pairs, cols), axe...  6.32 us
    pallas_call x1, Pallas kernels, analyse(): pl.pallas_call(functools.partial(analyse_kernel, spans), out_shape=struct...  5.58 us
    all_to_all x1, waiting for transfers between devices, per_device(): lax.all_to_all(outgoing.reshape(devices, owned * pairs, cols), axes, spli...  3.92 us
    pallas_call x1, Pallas kernels, per_device(): pl.pallas_call(synthesise_kernel, out_shape=struct((map_count, low_pairs,...  3.13 us
    pallas_call x1, Pallas kernels, per_device(): pl.pallas_call(functools.partial(harmonic_kernel, same, low_pairs), out_s...  2.91 us
    all_to_all x1, starting transfers between devices, per_device(): lax.all_to_all(synthesised.reshape(devices, owned * low_pairs, cols), axe...  2.58 us
    pallas_call x1, Pallas kernels, per_device(): pl.pallas_call(functools.partial(prepare_kernel, pairs), out_shape=[struc...  2.44 us
  transfers between devices with their start and end apart: 2, of which 2 were waited for; matrix products, arithmetic and copies ran while one was open for 2% of the time, Pallas kernels for 10%

profile of v8, /device:TPU:0, one launch (start us, length us, event | category | flops | bytes accessed | tf_op | source)
XLA Modules:
  0.0 37.2 jit_solution(11444522525041878098)
XLA Ops:
  0.0 5.6 %analyse.1 = bf16[256,256]{1,0:T(8,128)(2,1)} custom-call(s32[2]{0:T(128)} %hi_hbm.1, s32[1,128]{1,0:T(1,128)} %bitcast.22, bf16[128,16,16,128]{3,2,1,0:T(8,128)(2,1)} %bitcast.25), custom_call_target="tpu_custom_call" | custom-call | tf_op jit(solution)/shard_map/analyse/pallas_call | solution.py:353
  5.6 7.3 %all-to-all-start = ((bf16[32,8,256]{2,1,0:T(8,128)(2,1)}), bf16[32,8,256]{2,1,0:T(8,128)(2,1)S(1)}, u32[]{:S(2)}, u32[]{:S(2)}) async-start(bf16[32,8,256]{2,1,0:T(8,128)(2,1)} %bitcast.28), calls=%async_computation | async-start | bytes 262144 | tf_op jit(solution)/shard_map/all_to_all | solution.py:388
  12.9 0.7 %dynamic_slice.3.own_ref = s32[4]{0:T(128)S(1)} dynamic-slice(s32[128]{0:T(128)} %param.10, s32[]{:T(128)S(6)} %select_n.3), dynamic_slice_sizes={4} | dynamic-slice | bytes 36 | tf_op jit(solution)/shard_map/dynamic_slice | solution.py:393
  13.7 0.0 copy-start
  13.7 0.7 %copy-done = f32[3072]{0:T(1024)S(1)} copy-done((f32[3072]{0:T(1024)S(1)}, f32[3072]{0:T(1024)}, u32[]{:S(2)}) %copy-start) | copy-done | bytes 12312
  14.4 2.4 %prepare.1 = (f32[4,1,3072]{2,1,0:T(1,128)S(1)}, bf16[4,1,3072]{2,1,0:T(2,128)(2,1)S(1)}, bf16[256,256]{1,0:T(8,128)(2,1)S(1)}, bf16[4,64,3072]{2,1,0:T(8,128)(2,1)S(1)}, bf16[4,64,3072]{2,1,0:T(8,128)(2,1)S(1)}) custom-call(s32[4]{0:T(128)S(1)} %dynamic_slice.3.own_ref, f32[1,3072]{1,0:T(1,128)S(1)} %bitcast.21, bf16[4,64,3072]{2,1,0:T(8,128)(2,1)} %bitcast.26, ...), custom_call_target="tpu_custom_call" | custom-call | flops 3145728 | bytes 3145728 | tf_op jit(solution)/shard_map/prepare/pallas_call | solution.py:397
  16.8 3.9 %all-to-all-done = bf16[32,8,256]{2,1,0:T(8,128)(2,1)S(1)} async-done(((bf16[32,8,256]{2,1,0:T(8,128)(2,1)}), bf16[32,8,256]{2,1,0:T(8,128)(2,1)S(1)}, u32[]{:S(2)}, u32[]{:S(2)}) %all-to-all-start) | async-done | bytes 131104 | tf_op jit(solution)/shard_map/all_to_all | solution.py:388
  20.7 0.0 copy-start.1
  20.7 0.0 copy-start.2
  20.7 2.9 %harmonic.1 = bf16[256,256]{1,0:T(8,128)(2,1)} custom-call(bf16[256,256]{1,0:T(8,128)(2,1)S(1)} %bitcast.19, f32[4,1,3072]{2,1,0:T(1,128)S(1)} %get-tuple-element.18.weight_ref, bf16[4,1,3072]{2,1,0:T(2,128)(2,1)S(1)} %get-tuple-element.19.sign_ref, bf16[256,256]{1,0:T(8,128)(2,1)S(1)} %get-tuple-element.20.gather_ref, ...), custom_call_target="tpu_custom_call" | custom-call | tf_op jit(solution)/shard_map/harmonic/pallas_call | solution.py:415
  23.6 2.6 %all-to-all-start.1 = ((bf16[32,8,256]{2,1,0:T(8,128)(2,1)}), bf16[32,8,256]{2,1,0:T(8,128)(2,1)S(1)}, u32[]{:S(2)}, u32[]{:S(2)}) async-start(bf16[32,8,256]{2,1,0:T(8,128)(2,1)} %bitcast.10), calls=%async_computation.1 | async-start | bytes 262144 | tf_op jit(solution)/shard_map/all_to_all | solution.py:424
  26.2 0.0 copy-done.1
  26.2 0.1 copy.8.column_ref
  26.4 0.0 copy-done.2
  26.4 1.4 %inverse_table.1 = (bf16[256,1024]{1,0:T(8,128)(2,1)S(1)}, bf16[256,1024]{1,0:T(8,128)(2,1)S(1)}, bf16[256,256]{1,0:T(8,128)(2,1)S(1)}, f32[2,2,8,128]{3,2,1,0:T(8,128)S(1)}) custom-call(s32[2]{0:T(128)S(1)} %copy-done.2, s32[1,128]{1,0:T(1,128)S(1)} %bitcast.24, s32[128,1]{1,0:T(8,128)S(1)} %copy.8.column_ref), custom_call_target="tpu_custom_call" | custom-call | flops 8388608 | bytes 1048576 | tf_op jit(solution)/shard_map/inverse_table/pallas_call | solution.py:434
  27.7 6.3 %all-to-all-done.1 = bf16[32,8,256]{2,1,0:T(8,128)(2,1)S(1)} async-done(((bf16[32,8,256]{2,1,0:T(8,128)(2,1)}), bf16[32,8,256]{2,1,0:T(8,128)(2,1)S(1)}, u32[]{:S(2)}, u32[]{:S(2)}) %all-to-all-start.1) | async-done | bytes 131104 | tf_op jit(solution)/shard_map/all_to_all | solution.py:424
  34.0 3.1 %synthesise.1 = f32[64,2,8,8,128]{4,3,2,1,0:T(8,128)} custom-call(f32[2,2,8,128]{3,2,1,0:T(8,128)S(1)} %get-tuple-element.14.phase_ref, bf16[256,1024]{1,0:T(8,128)(2,1)S(1)} %get-tuple-element.15.table_ref, bf16[256,1024]{1,0:T(8,128)(2,1)S(1)} %get-tuple-element.16.residue_ref, bf16[256,256]{1,0:T(8,128)(2,1)S(1)} %get-tuple-element.17.gather_ref, ...), custom_call_target="tpu_custom_call" | custom-call | tf_op jit(solution)/shard_map/synthesise/pallas_call | solution.py:456
Async XLA Ops:
  5.6 15.1 %all-to-all-start = ((bf16[32,8,256]{2,1,0:T(8,128)(2,1)}), bf16[32,8,256]{2,1,0:T(8,128)(2,1)S(1)}, u32[]{:S(2)}, u32[]{:S(2)}) async-start(bf16[32,8,256]{2,1,0:T(8,128)(2,1)} %bitcast.28), calls=%async_computation | async-start | bytes 262144 | tf_op jit(solution)/shard_map/all_to_all | solution.py:388
  13.7 0.7 %copy-start = (f32[3072]{0:T(1024)S(1)}, f32[3072]{0:T(1024)}, u32[]{:S(2)}) copy-start(f32[3072]{0:T(1024)} %param.13) | copy-start | bytes 36868
  20.7 5.5 %copy-start.1 = (s32[128]{0:T(128)S(1)}, s32[128]{0:T(128)}, u32[]{:S(2)}) copy-start(s32[128]{0:T(128)} %param.10) | copy-start | bytes 1540
  20.7 5.6 %copy-start.2 = (s32[2]{0:T(128)S(1)}, s32[2]{0:T(128)}, u32[]{:S(2)}) copy-start(s32[2]{0:T(128)} %lo_ref.1) | copy-start | bytes 28
  23.6 10.4 %all-to-all-start.1 = ((bf16[32,8,256]{2,1,0:T(8,128)(2,1)}), bf16[32,8,256]{2,1,0:T(8,128)(2,1)S(1)}, u32[]{:S(2)}, u32[]{:S(2)}) async-start(bf16[32,8,256]{2,1,0:T(8,128)(2,1)} %bitcast.10), calls=%async_computation.1 | async-start | bytes 262144 | tf_op jit(solution)/shard_map/all_to_all | solution.py:424
